TPU v7x, 32 devices: a whole 2x2x4 slice. The times are simulated.
32 devices in a mesh: pb: 8 (over z, x), ka: 4 (over y, core).
Axes of the slice: x: 2, y: 2, z: 4, core: 2. Of those that a mesh axis runs over, the one named last changes fastest.
Arguments:
- node_states: float32 [512, 256], P('pb'), may hold values from -17 to 17
- frames: float32 [12, 512], P(None, 'pb'), may hold values from -20 to 20, as said below
- edge_states: bfloat16 [512, 512, 128], P('pb', 'ka'), may hold values from -6 to 6
- chain_number: int32 [512], replicated, may hold values from 0 to 3, as said below
- residue_index: int32 [512], replicated, may hold values from 0 to 767, as said below
- padding_mask: int32 [512], replicated, may hold values from 0 to 1, as said below
- query_weight: bfloat16 [256, 2048], replicated, may hold values from -0.375 to 0.375
- key_weight: bfloat16 [256, 2048], replicated, may hold values from -0.375 to 0.375
- value_weight: bfloat16 [256, 2048], replicated, may hold values from -0.375 to 0.375
- point_query: bfloat16 [256, 192], replicated, may hold values from -0.375 to 0.375
- point_key: bfloat16 [256, 192], replicated, may hold values from -0.375 to 0.375
- point_value: bfloat16 [256, 288], replicated, may hold values from -0.375 to 0.375
- bias_weight: bfloat16 [128, 8], replicated, may hold values from -0.5 to 0.5
- point_gamma: float32 [8], replicated, may hold values from 0.3 to 3
- relpos_table: float32 [128, 128], replicated, may hold values from -3 to 3
- output_weight: bfloat16 [3456, 256], replicated, may hold values from -0.109375 to 0.109375
- attention_scales: float32 [256], replicated, may hold values from 0.5 to 1.5
- layer_project: bfloat16 [2, 256, 768], replicated, may hold values from -0.375 to 0.375
- layer_output: bfloat16 [2, 256, 256], replicated, may hold values from -0.375 to 0.375
- layer_expand: bfloat16 [2, 256, 256], replicated, may hold values from -0.375 to 0.375
- layer_shrink: bfloat16 [2, 256, 256], replicated, may hold values from -0.375 to 0.375
- layer_scales: float32 [2, 2, 256], replicated, may hold values from 0.5 to 1.5
- frame_weight: float32 [256, 6], replicated, may hold values from -0.375 to 0.375
- node_to_edge: bfloat16 [256, 768], replicated, may hold values from -0.375 to 0.375
- edge_first: bfloat16 [128, 384], replicated, may hold values from -0.5 to 0.5
- edge_second: bfloat16 [384, 384], replicated, may hold values from -0.3125 to 0.3125
- edge_third: bfloat16 [384, 128], replicated, may hold values from -0.3125 to 0.3125
- edge_biases: float32 [2, 384], replicated, may hold values from -3 to 3
- edge_scales: float32 [128], replicated, may hold values from 0.5 to 1.5
Outputs:
- node_out: float32 [512, 256], P('pb')
- frames_out: float32 [12, 512], P(None, 'pb')
- edges_out: bfloat16 [512, 512, 128], P('pb', 'ka')
Inputs may be any that keep to these rules, and one draw needn't show every extreme that they name: `chain_number`: never falls from one residue to the next; the first residue has 0 and the last 3. `residue_index`: rises by 1 or 2 from one residue to the next, starting at 0; exactly 256 of the rises are 2. `padding_mask`: the ones come first; at least 256 residues are ones and at least one is padding. `frames`: rows 0 to 8 form a proper rotation of each residue.
All inputs are finite; a program needn't handle non-finite values.
Results may differ from a plain program's by a relative error of at most 0.025.
Values may be sent and summed in bfloat16 or wider, within the bound.
A program may use at most 128 MiB of HBM per device.

v0:
```python
import functools
import math

import jax
import jax.numpy as jnp
import numpy as np
from jax import lax
from jax.experimental import pallas as pl
from jax.experimental.pallas import tpu as pltpu
from jax.sharding import PartitionSpec as P

C_S = 256
HEADS = 8
HD = 256
QKP = 8
VP = 12
EH = 384
RELBINS = 128
LAYERS = 2
TF_HD = 64


HIGHEST = lax.Precision.HIGHEST
NEG_FILL = -1000000000.0


def layer_norm(values, scales):
    centered = values - jnp.mean(values, axis=-1, keepdims=True)
    variance = jnp.mean(centered * centered, axis=-1, keepdims=True)
    return centered * lax.rsqrt(variance + 1e-05) * scales


def frame_parts(frames):
    rotation = jnp.transpose(frames[:9]).reshape(-1, 3, 3)
    offset = jnp.transpose(frames[9:12])
    return (rotation, offset)


def head_split(matrix, width):
    return matrix.reshape(matrix.shape[0], -1, width)


def lane_parts(count):
    width = HEADS * 3 * count
    padded = -(-width // 128) * 128
    lane = np.arange(padded)
    real = lane < width
    head, comp, point = lane // (3 * count), lane // count % 3, lane % count
    return padded, real, head, comp, point


def pick(sources, size, dtype):
    sources = jnp.asarray(sources, jnp.int32)
    return (jnp.arange(size, dtype=jnp.int32)[:, None] == sources[None, :]).astype(dtype)


def component_copies(count, size, dtype):
    padded, real, head, comp, point = lane_parts(count)
    copies = [np.where(real, (head * 3 + d) * count + point, -1) for d in range(3)]
    return pick(np.concatenate(copies), size, dtype)


def rotation_lanes(rotation, count, inverse):
    padded, real, head, comp, point = lane_parts(count)
    entries = [np.where(real, d * 3 + comp if inverse else comp * 3 + d, -1) for d in range(3)]
    return jnp.dot(
        rotation, pick(np.concatenate(entries), 9, jnp.float32), precision=HIGHEST
    )


def offset_lanes(offset, count):
    padded, real, head, comp, point = lane_parts(count)
    return jnp.dot(offset, pick(np.where(real, comp, -1), 3, jnp.float32), precision=HIGHEST)


def head_lanes(count):
    padded, real, head, comp, point = lane_parts(count)
    return pick(np.where(real, head, -1), HEADS, jnp.float32)


def add_thirds(values):
    third = values.shape[1] // 3
    return values[:, :third] + values[:, third : 2 * third] + values[:, 2 * third :]


def place_points(features, weight, rotation, offset, count):
    copies = component_copies(count, weight.shape[1], weight.dtype)
    spread = jnp.dot(weight, copies, preferred_element_type=jnp.float32).astype(weight.dtype)
    local = jnp.dot(features, spread, preferred_element_type=jnp.float32)
    return add_thirds(local * rotation_lanes(rotation, count, False)) + offset_lanes(offset, count)


def relative_bins(chain_rows, index_rows, chain_cols, index_cols):
    reach = (RELBINS - 2) // 2
    gap_class = jnp.clip(index_rows[:, None] - index_cols[None, :], -reach, reach) + reach
    same_chain = chain_rows[:, None] == chain_cols[None, :]
    return jnp.where(same_chain, gap_class, RELBINS - 1)


def point_logits(
    queries, key_vectors, query_places, key_places, pair_rep, bias_weight, point_gamma
):
    scalar = jnp.einsum(
        "ihd,jhd->hij", queries, key_vectors, preferred_element_type=jnp.float32
    ) / math.sqrt(HD)
    pair_bias = jnp.einsum("ijc,ch->hij", pair_rep, bias_weight, preferred_element_type=jnp.float32)
    heads = head_lanes(QKP)
    query_square = lax.dot_general(
        heads, query_places * query_places, (((1,), (1,)), ((), ())), precision=HIGHEST
    )
    key_square = lax.dot_general(
        heads, key_places * key_places, (((1,), (1,)), ((), ())), precision=HIGHEST
    )
    by_head = (query_places[None] * heads[:, None, :]).reshape(-1, query_places.shape[1])
    cross = lax.dot_general(
        by_head, key_places, (((1,), (1,)), ((), ())), precision=HIGHEST
    ).reshape(HEADS, query_places.shape[0], -1)
    distance = query_square[:, :, None] + key_square[:, None, :] - 2.0 * cross
    weight_points = math.sqrt(2.0 / (9.0 * QKP))
    return math.sqrt(1.0 / 3.0) * (
        scalar + pair_bias - 0.5 * weight_points * point_gamma[:, None, None] * distance
    )


def ipa_features(merged, rotation, offset):
    points_first = merged.shape[1] - HEADS * 3 * VP
    padded, real, head, comp, point = lane_parts(VP)
    point_global = jnp.pad(
        merged[:, points_first:], ((0, 0), (0, padded - HEADS * 3 * VP))
    )
    moved = point_global - offset_lanes(offset, VP)
    rotated = jnp.dot(
        moved, component_copies(VP, padded, jnp.float32), precision=HIGHEST
    ) * rotation_lanes(rotation, VP, True)
    local = add_thirds(rotated)
    owner = np.where(real, head * VP + point, -1)
    same = jnp.transpose(pick(owner, HEADS * VP, jnp.float32))
    lengths = jnp.sqrt(jnp.dot(local * local, same, precision=HIGHEST) + 1e-08)
    return jnp.concatenate(
        [merged[:, :points_first], local[:, : HEADS * 3 * VP], lengths], axis=1
    )


def encoder_rows(states, key_value, fill, project, output, expand, shrink, scales):
    queries = jnp.dot(
        states.astype(jnp.bfloat16), project[:, :C_S], preferred_element_type=jnp.float32
    ).astype(jnp.bfloat16) * jnp.asarray(1.0 / math.sqrt(TF_HD), jnp.bfloat16)
    owner = lax.broadcasted_iota(jnp.int32, (1, C_S), 1) // TF_HD
    context = jnp.zeros(states.shape, jnp.float32)
    for head in range(C_S // TF_HD):
        mine = owner == head
        only = jnp.where(mine, 1.0, 0.0)
        scores = lax.dot_general(
            queries * only.astype(jnp.bfloat16),
            key_value[:, :C_S],
            (((1,), (1,)), ((), ())),
            preferred_element_type=jnp.float32,
        )
        scores = scores + fill
        weights = jnp.exp(scores - jnp.max(scores, axis=-1, keepdims=True))
        inverse = 1.0 / jnp.sum(weights, axis=-1, keepdims=True)
        mixed = jnp.dot(
            weights.astype(jnp.bfloat16),
            key_value[:, C_S:],
            preferred_element_type=jnp.float32,
        )
        context = context + mixed * (inverse * only)
    middle = layer_norm(
        states
        + jnp.dot(context.astype(jnp.bfloat16), output, preferred_element_type=jnp.float32),
        scales[0:1],
    )
    hidden = jnp.maximum(
        jnp.dot(middle.astype(jnp.bfloat16), expand, preferred_element_type=jnp.float32), 0.0
    ).astype(jnp.bfloat16)
    return layer_norm(
        middle + jnp.dot(hidden, shrink, preferred_element_type=jnp.float32), scales[1:2]
    )


def encoder_kernel(
    states_ref,
    fill_ref,
    project,
    output,
    expand,
    shrink,
    scales,
    to_edge,
    bias,
    second_ref,
    row_ref,
    key_ref,
    old,
    new,
    key_value,
):
    count = states_ref.shape[0]
    rows, keys = row_ref.shape[0], key_ref.shape[0]
    chunk = math.gcd(count, 128)

    def apply(states, layer):
        return encoder_rows(
            states,
            key_value[...],
            fill_ref[...],
            project[layer],
            output[layer],
            expand[layer],
            shrink[layer],
            scales[layer],
        )

    old[...] = states_ref[...].astype(jnp.float32)
    buffers = (old, new)
    for layer in range(LAYERS):
        source, target = buffers[layer % 2], buffers[(layer + 1) % 2]
        key_value[...] = jnp.dot(
            source[...].astype(jnp.bfloat16),
            project[layer][:, C_S:],
            preferred_element_type=jnp.float32,
        ).astype(jnp.bfloat16)
        if layer < LAYERS - 1:

            def step(index, carry):
                window = pl.ds(pl.multiple_of(index * chunk, chunk), chunk)
                target[window, :] = apply(source[window, :], layer)
                return carry

            lax.fori_loop(0, count // chunk, step, 0)
        else:
            row_first = pl.multiple_of(lax.axis_index("pb") * rows, rows)
            key_first = pl.multiple_of(lax.axis_index("ka") * keys, keys)
            second = apply(source[pl.ds(row_first, rows), :], layer)
            second_ref[...] = second
            row_ref[...] = jnp.dot(
                second.astype(jnp.bfloat16), to_edge[:, :EH], preferred_element_type=jnp.float32
            )
            final = apply(source[pl.ds(key_first, keys), :], layer)
            key_ref[...] = (
                jnp.dot(
                    final.astype(jnp.bfloat16), to_edge[:, EH:], preferred_element_type=jnp.float32
                )
                + bias[...]
            )


def encode(states, valid, rows, keys, project, output, expand, shrink, scales, to_edge, bias):
    fill = jnp.where(valid, 0.0, NEG_FILL)[None]
    count = states.shape[0]
    return pl.pallas_call(
        encoder_kernel,
        out_shape=(
            jax.ShapeDtypeStruct((rows, C_S), jnp.float32),
            jax.ShapeDtypeStruct((rows, EH), jnp.float32),
            jax.ShapeDtypeStruct((keys, EH), jnp.float32),
        ),
        in_specs=[pl.BlockSpec(memory_space=pltpu.VMEM)] * 9,
        out_specs=(pl.BlockSpec(memory_space=pltpu.VMEM),) * 3,
        scratch_shapes=[
            pltpu.VMEM((count, C_S), jnp.float32),
            pltpu.VMEM((count, C_S), jnp.float32),
            pltpu.VMEM((count, 2 * C_S), jnp.bfloat16),
        ],
    )(states, fill, project, output, expand, shrink, scales, to_edge, bias[None])


def update_frames(states, frames, frame_weight):
    update = jnp.dot(states, frame_weight, precision=HIGHEST)
    length = jnp.sqrt(
        1.0
        + update[:, 0] * update[:, 0]
        + update[:, 1] * update[:, 1]
        + update[:, 2] * update[:, 2]
    )
    real_part = 1.0 / length
    first_imag = update[:, 0] / length
    second_imag = update[:, 1] / length
    third_imag = update[:, 2] / length
    row_one = jnp.stack(
        [
            real_part * real_part
            + first_imag * first_imag
            - second_imag * second_imag
            - third_imag * third_imag,
            2.0 * (first_imag * second_imag - real_part * third_imag),
            2.0 * (first_imag * third_imag + real_part * second_imag),
        ],
        axis=1,
    )
    row_two = jnp.stack(
        [
            2.0 * (first_imag * second_imag + real_part * third_imag),
            real_part * real_part
            - first_imag * first_imag
            + second_imag * second_imag
            - third_imag * third_imag,
            2.0 * (second_imag * third_imag - real_part * first_imag),
        ],
        axis=1,
    )
    row_three = jnp.stack(
        [
            2.0 * (first_imag * third_imag - real_part * second_imag),
            2.0 * (second_imag * third_imag + real_part * first_imag),
            real_part * real_part
            - first_imag * first_imag
            - second_imag * second_imag
            + third_imag * third_imag,
        ],
        axis=1,
    )
    turn = jnp.stack([row_one, row_two, row_three], axis=1)
    rotation, offset = frame_parts(frames)
    new_rotation = jnp.einsum("rcd,rde->rce", rotation, turn, precision=HIGHEST)
    new_offset = jnp.einsum("rcd,rd->rc", rotation, update[:, 3:6], precision=HIGHEST) + offset
    return jnp.transpose(jnp.concatenate([new_rotation.reshape(-1, 9), new_offset], axis=1))


MESH = pl.DeviceIdType.MESH


def greet(peers):
    barrier = pltpu.get_barrier_semaphore()
    for peer in peers:
        pl.semaphore_signal(barrier, inc=1, device_id=peer, device_id_type=MESH)
    pl.semaphore_wait(barrier, len(peers))


def key_tile_kernel(n_pb, n_ka, x_ref, o_ref, send, recv, own):
    row, col = lax.axis_index("pb"), lax.axis_index("ka")
    per = n_pb // n_ka
    peers = [{"pb": lax.rem(row + d, n_pb)} for d in range(1, n_pb)]
    greet(peers)
    for slot in range(per):

        @pl.when(row == col * per + slot)
        def _():
            local = pltpu.make_async_copy(x_ref, o_ref.at[slot], own)
            local.start()
            copies = [
                pltpu.make_async_remote_copy(
                    src_ref=x_ref,
                    dst_ref=o_ref.at[slot],
                    send_sem=send.at[d],
                    recv_sem=recv.at[slot],
                    device_id=peer,
                    device_id_type=MESH,
                )
                for d, peer in enumerate(peers)
            ]
            for copy in copies:
                copy.start()
            for copy in copies:
                copy.wait_send()
            local.wait()

    for slot in range(per):

        @pl.when(row != col * per + slot)
        def _():
            pltpu.make_async_remote_copy(
                src_ref=x_ref,
                dst_ref=o_ref.at[slot],
                send_sem=send.at[0],
                recv_sem=recv.at[slot],
                device_id=peers[0],
                device_id_type=MESH,
            ).wait_recv()


def key_tile(packed, n_pb, n_ka):
    per = n_pb // n_ka
    return pl.pallas_call(
        functools.partial(key_tile_kernel, n_pb, n_ka),
        out_shape=jax.ShapeDtypeStruct((per,) + packed.shape, packed.dtype),
        in_specs=[pl.BlockSpec(memory_space=pltpu.VMEM)],
        out_specs=pl.BlockSpec(memory_space=pltpu.VMEM),
        scratch_shapes=[
            pltpu.SemaphoreType.DMA((n_pb - 1,)),
            pltpu.SemaphoreType.DMA((per,)),
            pltpu.SemaphoreType.DMA,
        ],
        compiler_params=pltpu.CompilerParams(collective_id=0, has_side_effects=True),
    )(packed)


def exchange_kernel(n_ka, sums_ref, stats_ref, sums_out, stats_out, send, recv, own):
    me = lax.axis_index("ka")
    peers = [lax.rem(me + d, n_ka) for d in range(1, n_ka)]
    greet([{"ka": peer} for peer in peers])
    copies = []
    for d, peer in enumerate(peers):
        for part, (source, target) in enumerate(((sums_ref, sums_out), (stats_ref, stats_out))):
            copy = pltpu.make_async_remote_copy(
                src_ref=source.at[peer],
                dst_ref=target.at[me],
                send_sem=send.at[2 * d + part],
                recv_sem=recv.at[2 * d + part],
                device_id={"ka": peer},
                device_id_type=MESH,
            )
            copy.start()
            copies.append(copy)
    for part, (source, target) in enumerate(((sums_ref, sums_out), (stats_ref, stats_out))):
        copy = pltpu.make_async_copy(source.at[me], target.at[me], own.at[part])
        copy.start()
        copies.append(copy)
    for copy in copies:
        copy.wait()


def exchange(sums, stats, n_ka):
    return pl.pallas_call(
        functools.partial(exchange_kernel, n_ka),
        out_shape=(
            jax.ShapeDtypeStruct(sums.shape, sums.dtype),
            jax.ShapeDtypeStruct(stats.shape, stats.dtype),
        ),
        in_specs=[pl.BlockSpec(memory_space=pltpu.VMEM)] * 2,
        out_specs=(pl.BlockSpec(memory_space=pltpu.VMEM),) * 2,
        scratch_shapes=[
            pltpu.SemaphoreType.DMA((2 * n_ka - 2,)),
            pltpu.SemaphoreType.DMA((2 * n_ka - 2,)),
            pltpu.SemaphoreType.DMA((2,)),
        ],
        compiler_params=pltpu.CompilerParams(collective_id=1, has_side_effects=True),
    )(sums, stats)


def gather_kernel(n_pb, n_ka, x_ref, o_ref, send, recv, own):
    row, col = lax.axis_index("pb"), lax.axis_index("ka")
    along_pb = [{"pb": lax.rem(row + d, n_pb)} for d in range(1, n_pb)]
    along_ka = [{"ka": lax.rem(col + d, n_ka)} for d in range(1, n_ka)]
    greet(along_pb + along_ka)
    copies = [pltpu.make_async_copy(x_ref, o_ref.at[col, row], own)] + [
        pltpu.make_async_remote_copy(
            src_ref=x_ref,
            dst_ref=o_ref.at[col, row],
            send_sem=send.at[d],
            recv_sem=recv.at[d],
            device_id=peer,
            device_id_type=MESH,
        )
        for d, peer in enumerate(along_pb)
    ]
    for copy in copies:
        copy.start()
    for copy in copies:
        copy.wait()
    copies = [
        pltpu.make_async_remote_copy(
            src_ref=o_ref.at[col],
            dst_ref=o_ref.at[col],
            send_sem=send.at[n_pb - 1 + d],
            recv_sem=recv.at[n_pb - 1 + d],
            device_id=peer,
            device_id_type=MESH,
        )
        for d, peer in enumerate(along_ka)
    ]
    for copy in copies:
        copy.start()
    for copy in copies:
        copy.wait()


def gather_rows(x, n_pb, n_ka):
    out = pl.pallas_call(
        functools.partial(gather_kernel, n_pb, n_ka),
        out_shape=jax.ShapeDtypeStruct((n_ka, n_pb) + x.shape, x.dtype),
        in_specs=[pl.BlockSpec(memory_space=pltpu.VMEM)],
        out_specs=pl.BlockSpec(memory_space=pltpu.VMEM),
        scratch_shapes=[
            pltpu.SemaphoreType.DMA((n_pb + n_ka - 2,)),
            pltpu.SemaphoreType.DMA((n_pb + n_ka - 2,)),
            pltpu.SemaphoreType.DMA,
        ],
        compiler_params=pltpu.CompilerParams(collective_id=2, has_side_effects=True),
    )(x)
    return jnp.transpose(out, (1, 0, 2, 3)).reshape(-1, x.shape[-1])


def edge_kernel(
    pair_ref, row_ref, key_ref, live_row, live_key, first, second, third, bias, scale, o_ref
):
    rows, keys, width = pair_ref.shape
    pair = pair_ref[...].reshape(rows * keys, width)
    hidden = jnp.dot(pair, first[...], preferred_element_type=jnp.float32)
    hidden = hidden.reshape(rows, keys, -1) + row_ref[...][:, None, :] + key_ref[...][None]
    hidden = jnp.maximum(hidden, 0.0).astype(jnp.bfloat16).reshape(rows * keys, -1)
    middle = jnp.dot(hidden, second[...], preferred_element_type=jnp.float32) + bias[...]
    middle = jnp.maximum(middle, 0.0).astype(jnp.bfloat16)
    result = pair.astype(jnp.float32) + jnp.dot(
        middle, third[...], preferred_element_type=jnp.float32
    )
    normed = layer_norm(result, scale[...]).reshape(rows, keys, width)
    live = live_row[...][:, None, :] * live_key[...][None]
    o_ref[...] = (normed * live).astype(o_ref.dtype)


def edge_transition(pair_rep, row_part, key_part, mask_rows, mask_keys, mats, bias, scale):
    rows, keys, width = pair_rep.shape
    step = 8
    live_row = jnp.broadcast_to(mask_rows.astype(jnp.float32)[:, None], (rows, width))
    live_key = jnp.broadcast_to(mask_keys.astype(jnp.float32)[:, None], (keys, width))

    def whole(array):
        return pl.BlockSpec(array.shape, lambda i: (0, 0))

    flat = [live_key, *mats, bias[None], scale[None]]
    return pl.pallas_call(
        edge_kernel,
        grid=(rows // step,),
        out_shape=jax.ShapeDtypeStruct(pair_rep.shape, jnp.bfloat16),
        in_specs=[
            pl.BlockSpec((step, keys, width), lambda i: (i, 0, 0)),
            pl.BlockSpec((step, row_part.shape[1]), lambda i: (i, 0)),
            whole(key_part),
            pl.BlockSpec((step, width), lambda i: (i, 0)),
        ]
        + [whole(array) for array in flat],
        out_specs=pl.BlockSpec((step, keys, width), lambda i: (i, 0, 0)),
    )(pair_rep, row_part, key_part, live_row, *flat)


def finish_rows(merged, rotation, offset, states, output_weight, attention_scales):
    features = ipa_features(merged, rotation, offset).astype(jnp.bfloat16)
    return layer_norm(
        states + jnp.dot(features, output_weight, preferred_element_type=jnp.float32),
        attention_scales,
    )


def on_device(
    node_states,
    frames,
    edge_states,
    chain_number,
    residue_index,
    padding_mask,
    query_weight,
    key_weight,
    value_weight,
    point_query,
    point_key,
    point_value,
    bias_weight,
    point_gamma,
    relpos_table,
    output_weight,
    attention_scales,
    layer_project,
    layer_output,
    layer_expand,
    layer_shrink,
    layer_scales,
    frame_weight,
    node_to_edge,
    edge_first,
    edge_second,
    edge_third,
    edge_biases,
    edge_scales,
):
    row_count = node_states.shape[0]
    key_count = edge_states.shape[1]
    row_first = lax.axis_index("pb") * row_count
    key_first = lax.axis_index("ka") * key_count
    n_pb, n_ka = lax.axis_size("pb"), lax.axis_size("ka")
    packed = jnp.concatenate([node_states, jnp.transpose(frames)], axis=1).astype(jnp.bfloat16)
    packed = jnp.pad(packed, ((0, 0), (0, -packed.shape[1] % 128)))
    tile = key_tile(packed, n_pb, n_ka).reshape(key_count, -1)
    key_input = tile[:, :C_S]
    key_rotation = tile[:, C_S : C_S + 9].astype(jnp.float32)
    key_offset = tile[:, C_S + 9 : C_S + 12].astype(jnp.float32)
    chain_rows = lax.dynamic_slice_in_dim(chain_number, row_first, row_count, 0)
    chain_keys = lax.dynamic_slice_in_dim(chain_number, key_first, key_count, 0)
    index_rows = lax.dynamic_slice_in_dim(residue_index, row_first, row_count, 0)
    index_keys = lax.dynamic_slice_in_dim(residue_index, key_first, key_count, 0)
    mask_rows = lax.dynamic_slice_in_dim(padding_mask, row_first, row_count, 0)
    mask_keys = lax.dynamic_slice_in_dim(padding_mask, key_first, key_count, 0)
    rotation, offset = jnp.transpose(frames[:9]), jnp.transpose(frames[9:12])
    row_input = node_states.astype(jnp.bfloat16)
    queries = head_split(
        jnp.dot(row_input, query_weight, preferred_element_type=jnp.float32).astype(jnp.bfloat16),
        HD,
    )
    key_vectors = head_split(
        jnp.dot(key_input, key_weight, preferred_element_type=jnp.float32).astype(jnp.bfloat16), HD
    )
    value_vectors = head_split(
        jnp.dot(key_input, value_weight, preferred_element_type=jnp.float32).astype(jnp.bfloat16),
        HD,
    )
    query_places = place_points(row_input, point_query, rotation, offset, QKP)
    key_places = place_points(key_input, point_key, key_rotation, key_offset, QKP)
    value_places = place_points(key_input, point_value, key_rotation, key_offset, VP)
    bins = relative_bins(chain_rows, index_rows, chain_keys, index_keys)
    onehot = (bins[:, :, None] == jnp.arange(RELBINS, dtype=jnp.int32)).astype(jnp.bfloat16)
    onehot = onehot.reshape(-1, RELBINS)
    table_top = lax.reduce_precision(relpos_table, 8, 7)
    table_high = table_top.astype(jnp.bfloat16)
    table_low = (relpos_table - table_top).astype(jnp.bfloat16)
    relative = (
        jnp.dot(onehot, table_high, preferred_element_type=jnp.float32)
        + jnp.dot(onehot, table_low, preferred_element_type=jnp.float32)
    ).reshape(row_count, key_count, -1)
    pair_rep = (edge_states.astype(jnp.float32) + relative).astype(jnp.bfloat16)
    logits = point_logits(
        queries, key_vectors, query_places, key_places, pair_rep, bias_weight, point_gamma
    )
    key_valid = (mask_keys == 1)[None, None, :]
    masked = jnp.where(key_valid, logits, NEG_FILL)
    local_top = jnp.max(masked, axis=-1)
    weights = jnp.where(key_valid, jnp.exp(masked - local_top[..., None]), 0.0)
    local_total = jnp.sum(weights, axis=-1)
    rounded = weights.astype(jnp.bfloat16)
    scalar_acc = jnp.einsum(
        "hij,jhd->ihd", rounded, value_vectors, preferred_element_type=jnp.float32
    )
    pair_acc = jnp.einsum("hij,ijc->ihc", rounded, pair_rep, preferred_element_type=jnp.float32)
    point_all = jnp.dot(
        weights.reshape(-1, key_count), value_places, precision=HIGHEST
    ).reshape(HEADS, row_count, -1)
    point_acc = jnp.sum(point_all * head_lanes(VP)[:, None, :], axis=0)
    part = row_count // n_ka
    sums = jnp.concatenate(
        [
            scalar_acc.reshape(row_count, -1),
            pair_acc.reshape(row_count, -1),
            point_acc[:, : HEADS * 3 * VP],
        ],
        axis=1,
    ).astype(jnp.bfloat16)
    used = sums.shape[1]
    sums = jnp.pad(sums, ((0, 0), (0, -used % 128))).reshape(n_ka, part, -1)
    stats = jnp.concatenate([jnp.transpose(local_top), jnp.transpose(local_total)], axis=1)
    stats = jnp.pad(stats, ((0, 0), (0, -stats.shape[1] % 128))).reshape(n_ka, part, -1)
    sums, stats = exchange(sums, stats, n_ka)
    tops, totals = stats[..., :HEADS], stats[..., HEADS : 2 * HEADS]
    factor = jnp.exp(tops - jnp.max(tops, axis=0))
    factor = factor / jnp.sum(totals * factor, axis=0)
    channels = pair_rep.shape[-1]
    spread = jnp.concatenate(
        [
            jnp.repeat(factor, HD, axis=2),
            jnp.repeat(factor, channels, axis=2),
            jnp.repeat(factor, 3 * VP, axis=2),
        ],
        axis=2,
    )
    merged = jnp.sum(sums[..., :used].astype(jnp.float32) * spread, axis=0)
    part_first = lax.axis_index("ka") * part
    first_states = finish_rows(
        merged,
        lax.dynamic_slice_in_dim(rotation, part_first, part, 0),
        lax.dynamic_slice_in_dim(offset, part_first, part, 0),
        lax.dynamic_slice_in_dim(node_states, part_first, part, 0),
        output_weight,
        attention_scales,
    )
    every_valid = padding_mask == 1
    whole_states = gather_rows(first_states.astype(jnp.bfloat16), n_pb, n_ka)
    second_states, row_project, key_project = encode(
        whole_states,
        every_valid,
        row_count,
        key_count,
        layer_project,
        layer_output,
        layer_expand,
        layer_shrink,
        layer_scales,
        node_to_edge,
        edge_biases[0],
    )
    frames_out = update_frames(second_states, frames, frame_weight)
    edges_out = edge_transition(
        pair_rep,
        row_project,
        key_project,
        mask_rows,
        mask_keys,
        (edge_first, edge_second, edge_third),
        edge_biases[1],
        edge_scales,
    )
    return (second_states, frames_out, edges_out)


def solution(mesh):
    placed = (
        P("pb", None),
        P(None, "pb"),
        P("pb", "ka", None),
        P(),
        P(),
        P(),
        P(),
        P(),
        P(),
        P(),
        P(),
        P(),
        P(),
        P(),
        P(),
        P(),
        P(),
        P(),
        P(),
        P(),
        P(),
        P(),
        P(),
        P(),
        P(),
        P(),
        P(),
        P(),
        P(),
    )
    return jax.shard_map(
        on_device,
        mesh=mesh,
        in_specs=placed,
        out_specs=(P("pb", None), P(None, "pb"), P("pb", "ka", None)),
        check_vma=False,
    )
```

profile of v0, /device:TPU:1, one launch (start us, length us, event | category | flops | bytes accessed | tf_op | source)
XLA Modules:
  0.0 106.4 jit_solution(1073070570438434381)
XLA Ops:
  0.7 0.9 dynamic_slice.26
  1.6 0.8 dynamic_slice.28
  2.4 0.8 dynamic_slice.25
  3.1 0.8 dynamic_slice.27
  4.0 2.2 %fusion = f32[8192,128]{1,0:T(8,128)S(1)} fusion(s32[8192]{0:T(1024)S(1)} %fusion.71, f32[128,128]{1,0:T(8,128)} %param.58), kind=kOutput, calls=%fused_computation.3 | convolution fusion | flops 269516800 | bytes 4292608 | tf_op jit(solution)/shard_map/dot_general | solution.py:606
  6.2 1.3 %convolution_add_fusion = f32[8192,128]{1,0:T(8,128)S(1)} fusion(f32[8192,128]{1,0:T(8,128)S(1)} %fusion, s32[8192]{0:T(1024)S(1)} %fusion.71, f32[128,128]{1,0:T(8,128)S(1)} %copy-done.8), kind=kOutput, calls=%fused_computation | convolution fusion | flops 270581760 | bytes 8486912 | tf_op jit(solution)/shard_map/dot_general | solution.py:607
  7.7 0.8 add_convert_fusion.pair_ref
  8.6 1.3 %copy-done.1 = bf16[64,128,128]{2,1,0:T(8,128)(2,1)} copy-done((bf16[64,128,128]{2,1,0:T(8,128)(2,1)}, bf16[64,128,128]{2,1,0:T(8,128)(2,1)S(1)}, u32[]{:S(2)}) %copy-start.1) | copy-done | bytes 2097176
  11.5 8.4 %shard_map.427 = bf16[2,64,384]{2,1,0:T(8,128)(2,1)} custom-call(bf16[64,384]{1,0:T(8,128)(2,1)} %fusion.59.x_ref), custom_call_target="tpu_custom_call" | custom-call | tf_op jit(solution)/shard_map/pallas_call | solution.py:374
  20.0 1.2 %convolution_convert_fusion.1 = bf16[128,2048]{1,0:T(8,128)(2,1)S(1)} fusion(bf16[256,2048]{1,0:T(8,128)(2,1)S(1)} %copy-done.5, bf16[128,384]{1,0:T(8,128)(2,1)} %bitcast.112), kind=kOutput, calls=%fused_computation.6 | convolution fusion | flops 134479872 | bytes 1638400 | tf_op jit(solution)/shard_map/dot_general | solution.py:590
  21.2 1.5 %convolution_convert_fusion.3 = bf16[64,2048]{1,0:T(8,128)(2,1)S(1)} fusion(bf16[64,256]{1,0:T(8,128)(2,1)S(1)} %convert.31, bf16[256,2048]{1,0:T(8,128)(2,1)} %param.50), kind=kOutput, calls=%fused_computation.8 | convolution fusion | flops 67239936 | bytes 1343488 | tf_op jit(solution)/shard_map/dot_general | solution.py:586
  22.8 1.0 fusion.15
  24.0 2.3 %fusion.8 = f32[128,768]{1,0:T(8,128)} fusion(f32[128,768]{1,0:T(8,128)S(1)} %fusion.60, bf16[256,192]{0,1:T(8,128)(2,1)} %param.54, s32[768]{0:T(1024)S(1)} %copy-done.18, bf16[128,384]{1,0:T(8,128)(2,1)S(1)} %bitcast.114), kind=kOutput, calls=%fused_computation.22 | convolution fusion | flops 126271488 | bytes 954368 | tf_op jit(solution)/shard_map/dot_general | solution.py:89
  26.3 1.2 %convolution_add_fusion.2 = f32[128,256]{1,0:T(8,128)S(1)} fusion(f32[128,768]{1,0:T(8,128)} %fusion.8, bf16[128,384]{1,0:T(8,128)(2,1)S(1)} %bitcast.115, s32[256]{0:T(256)S(1)} %copy-done.19), kind=kOutput, calls=%fused_computation.39 | convolution fusion | flops 295680 | bytes 558080 | tf_op jit(solution)/shard_map/dot_general | solution.py:73
  28.1 2.1 %fusion.17 = f32[64,768]{1,0:T(8,128)} fusion(f32[768,64]{0,1:T(8,128)S(1)} %fusion.61, bf16[64,256]{1,0:T(8,128)(2,1)S(1)} %convert.31, bf16[256,192]{0,1:T(8,128)(2,1)} %param.53, s32[768]{0:T(1024)S(1)} %copy-done.18), kind=kOutput, calls=%fused_computation.34 | convolution fusion | flops 101056512 | bytes 527360 | tf_op jit(solution)/shard_map/dot_general | solution.py:89
  30.2 1.1 %fusion.19 = f32[64,256]{1,0:T(8,128)S(1)} fusion(f32[64,768]{1,0:T(8,128)} %fusion.17, s32[256]{0:T(256)S(1)} %copy-done.19, f32[12,64]{1,0:T(8,128)S(1)} %copy-done.9), kind=kOutput, calls=%fused_computation.41 | convolution fusion | flops 639744 | bytes 265216 | tf_op jit(solution)/shard_map/dot_general | solution.py:73
  31.5 1.6 %fusion.98 = (f32[8,64]{1,0:T(8,128)S(1)}, f32[8,64,128]{2,1,0:T(8,128)S(1)}) fusion(f32[8,64,128]{2,1,0:T(8,128)} %fusion.15, f32[128,256]{1,0:T(8,128)S(1)} %convolution_add_fusion.2, f32[8,256]{1,0:T(8,128)S(1)} %fusion.82, f32[64,256]{1,0:T(8,128)S(1)} %fusion.19, f32[8,128]{1,0:T(8,128)S(1)} %fusion.50, f32[8,64]{1,0:T(8,128)S(1)} %fusion.57, ...), kind=kOutput, calls=%fused_computation.184 | convolution fusion | flops 201981440 | bytes 737440 | tf_op jit(solution)/shard_map/dot_general | solution.py:115
  35.8 1.9 %fusion.4 = f32[128,1152]{1,0:T(8,128)S(1)} fusion(bf16[256,288]{0,1:T(8,128)(2,1)} %param.55, s32[1152]{0:T(1024)S(1)} %copy-done.26, bf16[128,384]{1,0:T(8,128)(2,1)S(1)} %bitcast.117), kind=kOutput, calls=%fused_computation.16 | convolution fusion | flops 245993472 | bytes 811008 | tf_op jit(solution)/shard_map/dot_general | solution.py:89
  38.1 0.8 fusion.5
  39.0 0.8 fusion.35
  39.8 12.7 %shard_map.428 = (bf16[4,16,3456]{2,1,0:T(8,128)(2,1)}, f32[4,16,128]{2,1,0:T(8,128)}) custom-call(bf16[4,16,3456]{2,1,0:T(8,128)(2,1)} %bitcast.120, f32[4,16,128]{2,1,0:T(8,128)} %bitcast.129), custom_call_target="tpu_custom_call" | custom-call | tf_op jit(solution)/shard_map/pallas_call | solution.py:414
  52.5 0.8 slice_reduce_fusion
  53.4 0.9 multiply_reduce_fusion
  54.3 0.8 fusion.76
  56.2 0.7 fusion.3
  58.2 0.7 multiply_convert_fusion.x_ref
  58.9 12.8 %shard_map.429 = bf16[4,8,16,256]{3,2,1,0:T(8,128)(2,1)} custom-call(bf16[16,256]{1,0:T(8,128)(2,1)} %multiply_convert_fusion.x_ref), custom_call_target="tpu_custom_call" | custom-call | tf_op jit(solution)/shard_map/pallas_call | solution.py:469
  71.7 1.7 %copy.89 = bf16[8,4,16,256]{3,2,1,0:T(8,128)(2,1)} copy(bf16[8,4,16,256]{3,2,0,1:T(8,128)(2,1)} %bitcast.123) | data formatting | bytes 524288 | tf_op jit(solution)/shard_map/transpose | solution.py:481
  74.6 16.0 %shard_map.430 = (f32[64,256]{1,0:T(8,128)}, f32[64,384]{1,0:T(8,128)}, f32[128,384]{1,0:T(8,128)}) custom-call(bf16[512,256]{1,0:T(8,128)(2,1)} %bitcast.124, f32[1,512]{1,0:T(1,128)} %bitcast.134, bf16[2,256,768]{2,1,0:T(8,128)(2,1)} %project.1, bf16[2,256,256]{2,1,0:T(8,128)(2,1)} %output.1, bf16[2,256,256]{2,1,0:T(8,128)(2,1)} %expand.1, ...), custom_call_target="tpu_custom_call" | custom-call | tf_op jit(solution)/shard_map/pallas_call | solution.py:251
  90.6 0.7 broadcast_in_dim.53.live_key
  91.4 0.7 broadcast_in_dim.52.live_row
  92.1 12.4 %shard_map.431 = bf16[64,128,128]{2,1,0:T(8,128)(2,1)} custom-call(bf16[64,128,128]{2,1,0:T(8,128)(2,1)} %copy-done.1, f32[64,384]{1,0:T(8,128)} %get-tuple-element.11.row_ref, f32[128,384]{1,0:T(8,128)} %get-tuple-element.12.key_ref, f32[64,128]{1,0:T(8,128)} %broadcast_in_dim.52.live_row, f32[128,128]{1,0:T(8,128)} %broadcast_in_dim.53.live_key, ...), custom_call_target="tpu_custom_call" | custom-call | tf_op jit(solution)/shard_map/pallas_call | solution.py:512
  (123 shorter events, 11.5 us)
Async XLA Ops:
  0.6 56.9 %copy-start = (bf16[3456,256]{1,0:T(8,128)(2,1)S(1)}, bf16[3456,256]{1,0:T(8,128)(2,1)}, u32[]{:S(2)}) copy-start(bf16[3456,256]{1,0:T(8,128)(2,1)} %param.59) | copy-start | bytes 5308420
  4.0 2.2 %copy-start.8 = (f32[128,128]{1,0:T(8,128)S(1)}, f32[128,128]{1,0:T(8,128)}, u32[]{:S(2)}) copy-start(f32[128,128]{1,0:T(8,128)} %param.58) | copy-start | bytes 196612
  6.1 1.6 %copy-start.3 = (bf16[64,128,128]{2,1,0:T(8,128)(2,1)S(1)}, bf16[64,128,128]{2,1,0:T(8,128)(2,1)}, u32[]{:S(2)}) copy-start(bf16[64,128,128]{2,1,0:T(8,128)(2,1)} %param.46) | copy-start | bytes 6291460
  7.7 2.2 %copy-start.23 = (bf16[128,8]{0,1:T(8,128)(2,1)S(1)}, bf16[128,8]{0,1:T(8,128)(2,1)}, u32[]{:S(2)}) copy-start(bf16[128,8]{0,1:T(8,128)(2,1)} %param.56) | copy-start | bytes 6148
  8.6 1.3 %copy-start.1 = (bf16[64,128,128]{2,1,0:T(8,128)(2,1)}, bf16[64,128,128]{2,1,0:T(8,128)(2,1)S(1)}, u32[]{:S(2)}) copy-start(bf16[64,128,128]{2,1,0:T(8,128)(2,1)S(1)} %add_convert_fusion.pair_ref) | copy-start | bytes 6291460
  9.9 0.8 copy-start.10
  9.9 0.8 copy-start.9
  9.9 10.0 %copy-start.5 = (bf16[256,2048]{1,0:T(8,128)(2,1)S(1)}, bf16[256,2048]{1,0:T(8,128)(2,1)}, u32[]{:S(2)}) copy-start(bf16[256,2048]{1,0:T(8,128)(2,1)} %param.51) | copy-start | bytes 3145732
  19.9 3.8 %copy-start.4 = (bf16[2,64,384]{2,1,0:T(8,128)(2,1)S(1)}, bf16[2,64,384]{2,1,0:T(8,128)(2,1)}, u32[]{:S(2)}) copy-start(bf16[2,64,384]{2,1,0:T(8,128)(2,1)} %shard_map.427) | copy-start | bytes 294916
  19.9 3.8 %copy-start.12 = (s32[768]{0:T(1024)S(1)}, s32[768]{0:T(1024)}, u32[]{:S(2)}) copy-start(s32[768]{0:T(1024)} %constant.79.clone) | copy-start | bytes 9220
  20.0 4.0 %copy-start.18 = (s32[768]{0:T(1024)S(1)}, s32[768]{0:T(1024)}, u32[]{:S(2)}) copy-start(s32[768]{0:T(1024)} %constant.78.clone) | copy-start | bytes 9220
  21.2 5.1 %copy-start.19 = (s32[256]{0:T(256)S(1)}, s32[256]{0:T(256)}, u32[]{:S(2)}) copy-start(s32[256]{0:T(256)} %constant.80.clone) | copy-start | bytes 3076
  21.2 6.3 %copy-start.13 = (s32[256]{0:T(256)S(1)}, s32[256]{0:T(256)}, u32[]{:S(2)}) copy-start(s32[256]{0:T(256)} %constant.84.clone) | copy-start | bytes 3076
  21.2 6.5 %copy-start.22 = (s32[512]{0:T(512)S(1)}, s32[512]{0:T(512)}, u32[]{:S(2)}) copy-start(s32[512]{0:T(512)} %param.49) | copy-start | bytes 6148
  22.8 8.7 %copy-start.25 = (f32[8]{0:T(128)S(1)}, f32[8]{0:T(128)}, u32[]{:S(2)}) copy-start(f32[8]{0:T(128)} %param.57) | copy-start | bytes 100
  23.8 10.3 %copy-start.6 = (bf16[256,2048]{1,0:T(8,128)(2,1)S(1)}, bf16[256,2048]{1,0:T(8,128)(2,1)}, u32[]{:S(2)}) copy-start(bf16[256,2048]{1,0:T(8,128)(2,1)} %param.52) | copy-start | bytes 3145732
  33.5 1.6 %copy-start.2 = (bf16[64,128,128]{2,1,0:T(8,128)(2,1)S(1)}, bf16[64,128,128]{2,1,0:T(8,128)(2,1)}, u32[]{:S(2)}) copy-start(bf16[64,128,128]{2,1,0:T(8,128)(2,1)} %copy-done.1) | copy-start | bytes 6291460
  34.4 1.3 %copy-start.26 = (s32[1152]{0:T(1024)S(1)}, s32[1152]{0:T(1024)}, u32[]{:S(2)}) copy-start(s32[1152]{0:T(1024)} %constant.81.clone) | copy-start | bytes 13828
  34.7 3.0 %copy-start.14 = (s32[1152]{0:T(1024)S(1)}, s32[1152]{0:T(1024)}, u32[]{:S(2)}) copy-start(s32[1152]{0:T(1024)} %constant.82.clone) | copy-start | bytes 13828
  35.1 2.8 %copy-start.15 = (s32[384]{0:T(512)S(1)}, s32[384]{0:T(512)}, u32[]{:S(2)}) copy-start(s32[384]{0:T(512)} %constant.83.clone) | copy-start | bytes 4612
  35.7 2.4 %copy-start.21 = (s32[384]{0:T(512)S(1)}, s32[384]{0:T(512)}, u32[]{:S(2)}) copy-start(s32[384]{0:T(512)} %constant.85.clone) | copy-start | bytes 4612
  52.5 3.2 %copy-start.7 = (bf16[4,16,3456]{2,1,0:T(8,128)(2,1)S(1)}, bf16[4,16,3456]{2,1,0:T(8,128)(2,1)}, u32[]{:S(2)}) copy-start(bf16[4,16,3456]{2,1,0:T(8,128)(2,1)} %get-tuple-element.8) | copy-start | bytes 1327108
  55.2 1.7 %copy-start.17 = (s32[1152]{0:T(1024)S(1)}, s32[1152]{0:T(1024)}, u32[]{:S(2)}) copy-start(s32[1152]{0:T(1024)} %constant.86.clone) | copy-start | bytes 13828
  55.3 1.9 %copy-start.27 = (s32[384]{0:T(512)S(1)}, s32[384]{0:T(512)}, u32[]{:S(2)}) copy-start(s32[384]{0:T(512)} %constant.87.clone) | copy-start | bytes 4612
  55.8 2.5 %copy-start.24 = (f32[256]{0:T(256)S(1)}, f32[256]{0:T(256)}, u32[]{:S(2)}) copy-start(f32[256]{0:T(256)} %param.60) | copy-start | bytes 3076
  55.9 17.5 %copy-start.20 = (f32[2,384]{1,0:T(2,128)S(1)}, f32[2,384]{1,0:T(2,128)}, u32[]{:S(2)}) copy-start(f32[2,384]{1,0:T(2,128)} %param.71) | copy-start | bytes 9220
  92.1 12.4 %copy-start.11 = (f32[64,256]{1,0:T(8,128)S(1)}, f32[64,256]{1,0:T(8,128)}, u32[]{:S(2)}) copy-start(f32[64,256]{1,0:T(8,128)} %get-tuple-element.5) | copy-start | bytes 196612
  92.1 12.4 %copy-start.16 = (f32[256,6]{0,1:T(8,128)S(1)}, f32[256,6]{0,1:T(8,128)}, u32[]{:S(2)}) copy-start(f32[256,6]{0,1:T(8,128)} %param.66) | copy-start | bytes 18436
where the time goes:
time: 107 us; the launch traced here: 106 us
  Pallas kernels  62.3 us (58%)
  matrix products  23.9 us (22%)
  local copies, waits for them, and re-layouts  11.2 us (10%)
  other arithmetic  7.67 us (7%)
  between operations  1.33 us (1%)
    pallas_call x1, Pallas kernels, encode(): pl.pallas_call(encoder_kernel, out_shape=(jax.ShapeDtypeStruct((rows, C_S...  16 us
    pallas_call x1, Pallas kernels, gather_rows(): pl.pallas_call(functools.partial(gather_kernel, n_pb, n_ka), out_shape=ja...  12.8 us
    pallas_call x1, Pallas kernels, exchange(): pl.pallas_call(functools.partial(exchange_kernel, n_ka), out_shape=(jax.S...  12.7 us
    pallas_call x1, Pallas kernels, edge_transition(): pl.pallas_call(edge_kernel, grid=(rows // step,), out_shape=jax.ShapeDtyp...  12.4 us
    pallas_call x1, Pallas kernels, key_tile(): pl.pallas_call(functools.partial(key_tile_kernel, n_pb, n_ka), out_shape=...  8.41 us
    dot_general x3, matrix products, place_points(): local = jnp.dot(features, spread, preferred_element_type=jnp.float32)  6.27 us
    dot_general x4, matrix products, offset_lanes(): jnp.dot(offset, pick(np.where(real, comp, -1), 3, jnp.float32), precision...  2.87 us
    unnamed x58, local copies, waits for them, and re-layouts  2.47 us

commit v1 on v0

v1 whole, which is shorter than its diff:
```python
import functools
import math

import jax
import jax.numpy as jnp
import numpy as np
from jax import lax
from jax.experimental import pallas as pl
from jax.experimental.pallas import tpu as pltpu
from jax.sharding import PartitionSpec as P

C_S = 256
C_Z = 128
HEADS = 8
HD = 256
QKP = 8
VP = 12
EH = 384
RELBINS = 128
LAYERS = 2
TF_HD = 64
LANES = 128

HIGHEST = lax.Precision.HIGHEST
NEG_FILL = -1000000000.0
CHAIN_STEP = 65536.0
MESH = pl.DeviceIdType.MESH
VMEM = pl.BlockSpec(memory_space=pltpu.VMEM)
ANY = pl.BlockSpec(memory_space=pl.ANY)


def dot(a, b, **options):
    return jnp.dot(a, b, preferred_element_type=jnp.float32, **options)


def contract(a, b, a_dim, b_dim, **options):
    return lax.dot_general(
        a, b, (((a_dim,), (b_dim,)), ((), ())), preferred_element_type=jnp.float32, **options
    )


def iota(shape, dim):
    return lax.broadcasted_iota(jnp.int32, shape, dim)


def layer_norm(values, scales):
    centered = values - jnp.mean(values, axis=-1, keepdims=True)
    variance = jnp.mean(centered * centered, axis=-1, keepdims=True)
    return centered * lax.rsqrt(variance + 1e-05) * scales


def by_component(count):
    target = np.arange(3 * LANES)
    comp, rest = target // LANES, target % LANES
    source = (rest // count * 3 + comp) * count + rest % count
    source = np.where(rest < HEADS * count, source, -1)
    return np.arange(HEADS * 3 * count)[:, None] == source[None, :]


def frame_columns(frames):
    count = frames.shape[0]
    eye = (iota((count, LANES), 0) == iota((count, LANES), 1)).astype(jnp.float32)
    return contract(frames, eye, 0, 0, precision=HIGHEST)


def place(local, columns):
    parts = [local[:, LANES * d : LANES * (d + 1)] for d in range(3)]
    return jnp.concatenate(
        [
            sum(columns[:, 3 * c + d : 3 * c + d + 1] * parts[d] for d in range(3))
            + columns[:, 9 + c : 10 + c]
            for c in range(3)
        ],
        axis=1,
    )


def head_of_lane(count):
    lane = iota((HEADS, 3 * LANES), 1) % LANES
    return (lane // count == iota((HEADS, 3 * LANES), 0)).astype(jnp.float32)


def attend_kernel(
    n_pb,
    n_ka,
    node,
    frames,
    chain,
    index,
    mask,
    point_query,
    point_key,
    point_value,
    bias_weight,
    gamma,
    relpos,
    scales,
    perm_qk,
    perm_v,
    perm_vt,
    first,
    edge_hbm,
    wq_hbm,
    wk_hbm,
    wv_hbm,
    ow_hbm,
    states_out,
    pair_hbm,
    hidden_hbm,
    edge_s,
    pair_s,
    hidden_s,
    wq,
    wk,
    wv,
    ow,
    x_send,
    x_keys,
    f_keys,
    bias_s,
    work_s,
    stats_send,
    stats_recv,
    part_send,
    part_recv,
    columns_s,
    node_s,
    mine,
    load_sem,
    store_sem,
    x_send_sem,
    x_recv_sem,
    f_send_sem,
    f_recv_sem,
    s_send_sem,
    s_recv_sem,
    p_send_sem,
    p_recv_sem,
    g_send_sem,
    g_recv_sem,
    h_send_sem,
    h_recv_sem,
):
    rows, keys, channels = edge_s.shape
    count = chain.shape[1]
    part = rows // n_ka
    per = n_pb // n_ka
    row, col = lax.axis_index("pb"), lax.axis_index("ka")
    along_pb = [{"pb": lax.rem(row + d, n_pb)} for d in range(1, n_pb)]
    others = [lax.rem(col + d, n_ka) for d in range(1, n_ka)]
    along_ka = [{"ka": other} for other in others]

    barrier = pltpu.get_barrier_semaphore()
    for peer in along_pb + along_ka:
        pl.semaphore_signal(barrier, inc=1, device_id=peer, device_id_type=MESH)
    loads = [
        pltpu.make_async_copy(source, target, load_sem.at[k])
        for k, (source, target) in enumerate(
            ((edge_hbm, edge_s), (wq_hbm, wq), (wk_hbm, wk), (wv_hbm, wv), (ow_hbm, ow))
        )
    ]
    for load in loads:
        load.start()

    x_send[...] = node[...].astype(jnp.bfloat16)

    code = chain[...].astype(jnp.float32) * CHAIN_STEP + index[...].astype(jnp.float32)
    code = jnp.broadcast_to(code, (8, count))
    at_row = iota((count, LANES), 0) == row * rows + iota((count, LANES), 1)
    row_code = dot(code, at_row.astype(jnp.float32), precision=HIGHEST)[0:1]
    at_key = iota((keys, count), 1) == col * keys + iota((keys, count), 0)
    key_code = contract(at_key.astype(jnp.float32), code, 1, 1, precision=HIGHEST)[:, 0:1]
    reach = (RELBINS - 2) // 2
    gap = row_code - key_code
    bins = jnp.where(
        jnp.abs(gap) < CHAIN_STEP / 2, jnp.clip(gap, -reach, reach) + reach, RELBINS - 1.0
    )
    table = relpos[...]
    high = table.astype(jnp.bfloat16)
    low = (table - high.astype(jnp.float32)).astype(jnp.bfloat16)
    table = jnp.concatenate([high, low], axis=1)
    bin_lane = iota((keys, RELBINS), 1).astype(jnp.float32)
    eye = (iota((channels, channels), 0) == iota((channels, channels), 1)).astype(jnp.bfloat16)
    bias_rows = contract(bias_weight[...], eye, 0, 0).astype(jnp.bfloat16)
    loads[0].wait()

    def pair_rows(start, size):
        onehot = jnp.concatenate(
            [
                jnp.where(bins[:, i : i + 1] == bin_lane, 1.0, 0.0).astype(jnp.bfloat16)
                for i in range(start, start + size)
            ],
            axis=0,
        )
        relative = dot(onehot, table)
        relative = relative[:, :channels] + relative[:, channels:]
        values = edge_s[start : start + size].astype(jnp.float32).reshape(size * keys, channels)
        values = (values + relative).astype(jnp.bfloat16)
        pair_s[start : start + size] = values.reshape(size, keys, channels)
        for i in range(size):
            bias_s[(start + i) * HEADS : (start + i + 1) * HEADS, :] = contract(
                bias_rows, values[i * keys : (i + 1) * keys], 1, 1
            )

    group = 8
    starts = list(range(0, rows, group))
    early = starts[: len(starts) // 2]
    late = starts[len(starts) // 2 :]
    for start in early:
        pair_rows(start, group)

    pl.semaphore_wait(barrier, len(along_pb) + len(along_ka))
    for slot in range(per):

        @pl.when(row == col * per + slot)
        def _():
            copies = []
            for d, peer in enumerate(along_pb):
                copies.append(
                    pltpu.make_async_remote_copy(
                        src_ref=x_send,
                        dst_ref=x_keys.at[slot],
                        send_sem=x_send_sem.at[d],
                        recv_sem=x_recv_sem.at[slot],
                        device_id=peer,
                        device_id_type=MESH,
                    )
                )
                copies.append(
                    pltpu.make_async_remote_copy(
                        src_ref=frames,
                        dst_ref=f_keys.at[slot],
                        send_sem=f_send_sem.at[d],
                        recv_sem=f_recv_sem.at[slot],
                        device_id=peer,
                        device_id_type=MESH,
                    )
                )
            for copy in copies:
                copy.start()
            x_keys[slot] = x_send[...]
            f_keys[slot] = frames[...]

    for start in late:
        pair_rows(start, group)
    pair_store = pltpu.make_async_copy(pair_s, pair_hbm, store_sem.at[0])
    pair_store.start()

    own_columns = frame_columns(frames[...])
    for a in range(n_ka):
        columns_s[a] = own_columns[a * part : (a + 1) * part]
        node_s[a] = node[a * part : (a + 1) * part, :]
    own = x_send[...]
    loads[1].wait()
    queries = dot(own, wq[...]).astype(jnp.bfloat16)
    spread = dot(point_query[...], perm_qk[...]).astype(jnp.bfloat16)
    query_places = place(dot(own, spread), own_columns)
    spread_key = dot(point_key[...], perm_qk[...]).astype(jnp.bfloat16)
    spread_value = dot(point_value[...], perm_v[...]).astype(jnp.bfloat16)
    heads_qk = head_of_lane(QKP)
    by_head = (query_places[:, None, :] * heads_qk[None]).reshape(rows * HEADS, 3 * LANES)
    query_square = jnp.sum(by_head * by_head, axis=-1, keepdims=True)

    for slot in range(per):

        @pl.when(row != col * per + slot)
        def _():
            pltpu.make_async_remote_copy(
                src_ref=x_send,
                dst_ref=x_keys.at[slot],
                send_sem=x_send_sem.at[0],
                recv_sem=x_recv_sem.at[slot],
                device_id=along_pb[0],
                device_id_type=MESH,
            ).wait_recv()
            pltpu.make_async_remote_copy(
                src_ref=frames,
                dst_ref=f_keys.at[slot],
                send_sem=f_send_sem.at[0],
                recv_sem=f_recv_sem.at[slot],
                device_id=along_pb[0],
                device_id_type=MESH,
            ).wait_recv()

    key_rows = jnp.concatenate([x_keys[slot] for slot in range(per)], axis=0)
    key_columns = jnp.concatenate([frame_columns(f_keys[slot]) for slot in range(per)], axis=0)
    key_places = place(dot(key_rows, spread_key), key_columns)
    cross = contract(by_head, key_places, 1, 1, precision=HIGHEST)
    key_square = contract(heads_qk, key_places * key_places, 1, 1, precision=HIGHEST)
    loads[2].wait()
    key_vectors = dot(key_rows, wk[...]).astype(jnp.bfloat16)
    for head in range(HEADS):
        window = slice(head * HD, (head + 1) * HD)
        work_s[pl.ds(head, rows, stride=HEADS), :] = contract(
            queries[:, window], key_vectors[:, window], 1, 1
        )
    own_head = iota((HEADS, HEADS), 0) == iota((HEADS, HEADS), 1)
    gammas = jnp.sum(jnp.where(own_head, gamma[...], 0.0), axis=1, keepdims=True)
    gammas = gammas * math.sqrt(2.0 / (9.0 * QKP))
    distance = (cross - 0.5 * query_square).reshape(rows, HEADS, keys) - 0.5 * key_square[None]
    logits = math.sqrt(1.0 / 3.0) * (
        work_s[...].reshape(rows, HEADS, keys) * (1.0 / math.sqrt(HD))
        + bias_s[...].reshape(rows, HEADS, keys)
        + gammas[None] * distance
    )
    key_first = pl.multiple_of(col * keys, keys)
    valid = (mask[0:1, pl.ds(key_first, keys)] == 1)[None]
    masked = jnp.where(valid, logits, NEG_FILL)
    top = jnp.max(masked, axis=-1, keepdims=True)
    weights = jnp.where(valid, jnp.exp(masked - top), 0.0)
    total = jnp.sum(weights, axis=-1, keepdims=True)
    lanes = stats_send.shape[-1]
    at_lane = iota((rows, 1, lanes), 0) == iota((rows, 1, lanes), 2)
    stats_send[0] = jnp.sum(jnp.where(at_lane, top, 0.0), axis=0)
    stats_send[1] = jnp.sum(jnp.where(at_lane, total, 0.0), axis=0)
    stats = [
        pltpu.make_async_remote_copy(
            src_ref=stats_send,
            dst_ref=stats_recv.at[d],
            send_sem=s_send_sem.at[d],
            recv_sem=s_recv_sem.at[d],
            device_id=peer,
            device_id_type=MESH,
        )
        for d, peer in enumerate(along_ka)
    ]
    for copy in stats:
        copy.start()

    work_s[...] = weights.reshape(rows * HEADS, keys)
    rounded = weights.astype(jnp.bfloat16)
    loads[3].wait()
    value_vectors = dot(key_rows, wv[...]).astype(jnp.bfloat16)
    scalar = [
        dot(
            work_s[pl.ds(head, rows, stride=HEADS), :].astype(jnp.bfloat16),
            value_vectors[:, head * HD : (head + 1) * HD],
        )
        for head in range(HEADS)
    ]
    pair_out = jnp.stack([dot(rounded[i], pair_s[i]) for i in range(rows)], axis=0)
    value_places = place(dot(key_rows, spread_value), key_columns)
    heads_v = head_of_lane(VP)
    points = dot(weights.reshape(rows * HEADS, keys), value_places, precision=HIGHEST)

    for copy in stats:
        copy.wait()
    highest = stats_send[0]
    for d in range(n_ka - 1):
        highest = jnp.maximum(highest, stats_recv[d, 0])
    share = jnp.exp(stats_send[0] - highest)
    whole = stats_send[1] * share
    for d in range(n_ka - 1):
        whole = whole + stats_recv[d, 1] * jnp.exp(stats_recv[d, 0] - highest)
    real_row = iota(whole.shape, 1) < rows
    share = jnp.where(real_row, share / jnp.where(real_row, whole, 1.0), 0.0)
    factor = jnp.sum(jnp.where(at_lane, share[None], 0.0), axis=-1, keepdims=True)
    bias_s[...] = jnp.broadcast_to(factor, (rows, HEADS, keys)).reshape(rows * HEADS, keys)
    work_s[...] = (pair_out * factor).reshape(rows * HEADS, channels)
    loads[4].wait()
    features = []
    for head in range(HEADS):
        scale = bias_s[pl.ds(head, rows, stride=HEADS), :]
        for half in range(HD // LANES):
            features.append(scalar[head][:, half * LANES : (half + 1) * LANES] * scale)
    for head in range(HEADS):
        features.append(work_s[pl.ds(head, rows, stride=HEADS), :])
    features = jnp.concatenate([piece.astype(jnp.bfloat16) for piece in features], axis=1)
    partial = dot(features, ow[: features.shape[1], :])
    points = points.reshape(rows, HEADS, 3 * LANES) * (heads_v[None] * factor)
    points = jnp.sum(points, axis=1)
    partial = jnp.concatenate([partial, points], axis=1)
    for a in range(n_ka):
        part_send[a] = partial[a * part : (a + 1) * part].astype(jnp.bfloat16)
    parts = [
        pltpu.make_async_remote_copy(
            src_ref=part_send.at[other],
            dst_ref=part_recv.at[d],
            send_sem=p_send_sem.at[d],
            recv_sem=p_recv_sem.at[d],
            device_id={"ka": other},
            device_id_type=MESH,
        )
        for d, other in enumerate(others)
    ]
    for copy in parts:
        copy.start()

    def hidden_rows(start):
        pair = pair_s[start : start + group].reshape(group * keys, channels)
        values = dot(pair, first[...]).astype(jnp.bfloat16)
        hidden_s[start : start + group] = values.reshape(group, keys, EH)
        store = pltpu.make_async_copy(
            hidden_s.at[pl.ds(start, group)],
            hidden_hbm.at[pl.ds(start, group)],
            store_sem.at[1 + start // group],
        )
        store.start()
        return store

    third = -(-len(starts) // 3)
    stores = [hidden_rows(start) for start in starts[:third]]
    value_base = HEADS * (HD + C_Z)
    point_weight = dot(perm_vt[...], ow[value_base : value_base + HEADS * 3 * VP, :]).astype(
        jnp.bfloat16
    )
    for copy in parts:
        copy.wait()
    merged = part_send[col].astype(jnp.float32)
    for d in range(n_ka - 1):
        merged = merged + part_recv[d].astype(jnp.float32)
    columns = columns_s[col]
    moved = [
        merged[:, C_S + LANES * c : C_S + LANES * (c + 1)] - columns[:, 9 + c : 10 + c]
        for c in range(3)
    ]
    local = [
        sum(columns[:, 3 * c + d : 3 * c + d + 1] * moved[c] for c in range(3)) for d in range(3)
    ]
    lengths = jnp.sqrt(sum(piece * piece for piece in local) + 1e-08)
    local = jnp.concatenate([piece.astype(jnp.bfloat16) for piece in local], axis=1)
    length_weight = ow[value_base + HEADS * 3 * VP :, :]
    states = (
        node_s[col]
        + merged[:, :C_S]
        + dot(local, point_weight)
        + dot(lengths[:, : HEADS * VP].astype(jnp.bfloat16), length_weight)
    )
    mine[...] = layer_norm(states, scales[...]).astype(jnp.bfloat16)
    states_out[row, col] = mine[...]
    gathers = [
        pltpu.make_async_remote_copy(
            src_ref=mine,
            dst_ref=states_out.at[row, col],
            send_sem=g_send_sem.at[d],
            recv_sem=g_recv_sem.at[d],
            device_id=peer,
            device_id_type=MESH,
        )
        for d, peer in enumerate(along_pb)
    ]
    for copy in gathers:
        copy.start()
    stores += [hidden_rows(start) for start in starts[third : 2 * third]]
    for copy in gathers:
        copy.wait()
    spreads = [
        pltpu.make_async_remote_copy(
            src_ref=states_out.at[:, col],
            dst_ref=states_out.at[:, col],
            send_sem=h_send_sem.at[d],
            recv_sem=h_recv_sem.at[d],
            device_id=peer,
            device_id_type=MESH,
        )
        for d, peer in enumerate(along_ka)
    ]
    for copy in spreads:
        copy.start()
    stores += [hidden_rows(start) for start in starts[2 * third :]]
    for slot in range(per):

        @pl.when(row == col * per + slot)
        def _():
            for d, peer in enumerate(along_pb):
                pltpu.make_async_remote_copy(
                    src_ref=x_send,
                    dst_ref=x_keys.at[slot],
                    send_sem=x_send_sem.at[d],
                    recv_sem=x_recv_sem.at[slot],
                    device_id=peer,
                    device_id_type=MESH,
                ).wait_send()
                pltpu.make_async_remote_copy(
                    src_ref=frames,
                    dst_ref=f_keys.at[slot],
                    send_sem=f_send_sem.at[d],
                    recv_sem=f_recv_sem.at[slot],
                    device_id=peer,
                    device_id_type=MESH,
                ).wait_send()

    for copy in spreads:
        copy.wait()
    pair_store.wait()
    for store in stores:
        store.wait()


def attend(n_pb, n_ka, small, large):
    node, frames, edge = small[0], small[1], large[0]
    rows, keys, channels = edge.shape
    part, per = rows // n_ka, n_pb // n_ka
    lanes = -(-rows // LANES) * LANES
    bf16, f32 = jnp.bfloat16, jnp.float32
    dma = pltpu.SemaphoreType.DMA
    return pl.pallas_call(
        functools.partial(attend_kernel, n_pb, n_ka),
        out_shape=(
            jax.ShapeDtypeStruct((n_pb, n_ka, part, C_S), bf16),
            jax.ShapeDtypeStruct(edge.shape, bf16),
            jax.ShapeDtypeStruct((rows, keys, EH), bf16),
        ),
        in_specs=[VMEM] * len(small) + [ANY] * len(large),
        out_specs=(VMEM, ANY, ANY),
        scratch_shapes=[
            pltpu.VMEM(edge.shape, bf16),
            pltpu.VMEM(edge.shape, bf16),
            pltpu.VMEM((rows, keys, EH), bf16),
            *[pltpu.VMEM(array.shape, bf16) for array in large[1:]],
            pltpu.VMEM((rows, C_S), bf16),
            pltpu.VMEM((per, rows, C_S), bf16),
            pltpu.VMEM((per,) + frames.shape, f32),
            pltpu.VMEM((rows * HEADS, keys), f32),
            pltpu.VMEM((rows * HEADS, keys), f32),
            pltpu.VMEM((2, HEADS, lanes), f32),
            pltpu.VMEM((n_ka - 1, 2, HEADS, lanes), f32),
            pltpu.VMEM((n_ka, part, C_S + 3 * LANES), bf16),
            pltpu.VMEM((n_ka - 1, part, C_S + 3 * LANES), bf16),
            pltpu.VMEM((n_ka, part, LANES), f32),
            pltpu.VMEM((n_ka, part, C_S), f32),
            pltpu.VMEM((part, C_S), bf16),
            dma((len(large),)),
            dma((1 + rows // 8,)),
            dma((n_pb - 1,)),
            dma((per,)),
            dma((n_pb - 1,)),
            dma((per,)),
            dma((n_ka - 1,)),
            dma((n_ka - 1,)),
            dma((n_ka - 1,)),
            dma((n_ka - 1,)),
            dma((n_pb - 1,)),
            dma((n_pb - 1,)),
            dma((n_ka - 1,)),
            dma((n_ka - 1,)),
        ],
        compiler_params=pltpu.CompilerParams(
            collective_id=0, has_side_effects=True, vmem_limit_bytes=40 << 20
        ),
    )(*small, *large)


def encoder_rows(states, key_value, fill, project, output, expand, shrink, scales):
    queries = dot(states.astype(jnp.bfloat16), project[:, :C_S]).astype(
        jnp.bfloat16
    ) * jnp.asarray(1.0 / math.sqrt(TF_HD), jnp.bfloat16)
    owner = iota((1, C_S), 1) // TF_HD
    context = jnp.zeros(states.shape, jnp.float32)
    for head in range(C_S // TF_HD):
        only = jnp.where(owner == head, 1.0, 0.0)
        scores = contract(queries * only.astype(jnp.bfloat16), key_value[:, :C_S], 1, 1) + fill
        weights = jnp.exp(scores - jnp.max(scores, axis=-1, keepdims=True))
        inverse = 1.0 / jnp.sum(weights, axis=-1, keepdims=True)
        mixed = dot(weights.astype(jnp.bfloat16), key_value[:, C_S:])
        context = context + mixed * (inverse * only)
    middle = layer_norm(states + dot(context.astype(jnp.bfloat16), output), scales[0:1])
    hidden = jnp.maximum(dot(middle.astype(jnp.bfloat16), expand), 0.0).astype(jnp.bfloat16)
    return layer_norm(middle + dot(hidden, shrink), scales[1:2])


def update_frames(states, frames, frame_weight):
    update = contract(frame_weight, states, 0, 1, precision=HIGHEST)
    x, y, z = update[0:1], update[1:2], update[2:3]
    length = jnp.sqrt(1.0 + x * x + y * y + z * z)
    w, x, y, z = 1.0 / length, x / length, y / length, z / length
    turn = (
        (w * w + x * x - y * y - z * z, 2.0 * (x * y - w * z), 2.0 * (x * z + w * y)),
        (2.0 * (x * y + w * z), w * w - x * x + y * y - z * z, 2.0 * (y * z - w * x)),
        (2.0 * (x * z - w * y), 2.0 * (y * z + w * x), w * w - x * x - y * y + z * z),
    )
    old = [frames[k : k + 1] for k in range(12)]
    rotation = [
        sum(old[3 * c + d] * turn[d][e] for d in range(3)) for c in range(3) for e in range(3)
    ]
    offset = [
        sum(old[3 * c + d] * update[3 + d : 4 + d] for d in range(3)) + old[9 + c]
        for c in range(3)
    ]
    return jnp.concatenate(rotation + offset, axis=0)


def finish_kernel(
    n_ka,
    hidden_ref,
    pair_ref,
    states_ref,
    mask,
    frames,
    project,
    output,
    expand,
    shrink,
    scales,
    frame_weight,
    to_edge,
    second,
    third,
    biases,
    edge_scale,
    node_out,
    frames_out,
    edges_out,
    row_part,
    key_part,
    live_row,
    live_key,
    states_s,
    key_value,
):
    step, keys, width = pair_ref.shape
    rows = node_out.shape[0]
    count = states_ref.shape[0]
    turn = pl.program_id(0)

    @pl.when(turn == 0)
    def _():
        row_first = pl.multiple_of(lax.axis_index("pb") * rows, rows)
        key_first = pl.multiple_of(lax.axis_index("ka") * keys, keys)
        fill = jnp.where(mask[...] == 1, 0.0, NEG_FILL)
        live = (mask[...] == 1).astype(jnp.bfloat16)
        live = jnp.broadcast_to(live, (16, count))
        at_row = (iota((rows, count), 1) == row_first + iota((rows, count), 0)).astype(jnp.bfloat16)
        at_key = (iota((keys, count), 1) == key_first + iota((keys, count), 0)).astype(jnp.bfloat16)
        live_row[...] = jnp.broadcast_to(contract(at_row, live, 1, 1)[:, 0:1], live_row.shape)
        live_key[...] = jnp.broadcast_to(contract(at_key, live, 1, 1)[:, 0:1], live_key.shape)

        def apply(states, layer):
            return encoder_rows(
                states,
                key_value[...],
                fill,
                project[layer],
                output[layer],
                expand[layer],
                shrink[layer],
                scales[layer],
            )

        key_value[...] = dot(states_ref[...], project[0][:, C_S:]).astype(jnp.bfloat16)
        chunk = math.gcd(count, 256)
        for start in range(0, count, chunk):
            window = slice(start, start + chunk)
            states_s[window, :] = apply(states_ref[window, :].astype(jnp.float32), 0)
        key_value[...] = dot(states_s[...].astype(jnp.bfloat16), project[1][:, C_S:]).astype(
            jnp.bfloat16
        )
        both = jnp.concatenate(
            [states_s[pl.ds(row_first, rows), :], states_s[pl.ds(key_first, keys), :]], axis=0
        )
        final = apply(both, 1)
        node_out[...] = final[:rows]
        row_part[...] = dot(final[:rows].astype(jnp.bfloat16), to_edge[:, :EH])
        key_part[...] = dot(final[rows:].astype(jnp.bfloat16), to_edge[:, EH:]) + biases[0:1]
        frames_out[...] = update_frames(final[:rows], frames[...], frame_weight[...])

    window = pl.ds(pl.multiple_of(turn * step, step), step)
    pair = pair_ref[...].reshape(step * keys, width)
    hidden = hidden_ref[...].astype(jnp.float32)
    hidden = hidden + row_part[window, :][:, None, :] + key_part[...][None]
    hidden = jnp.maximum(hidden, 0.0).astype(jnp.bfloat16).reshape(step * keys, -1)
    middle = dot(hidden, second[...]) + biases[1:2]
    middle = jnp.maximum(middle, 0.0).astype(jnp.bfloat16)
    result = pair.astype(jnp.float32) + dot(middle, third[...])
    normed = layer_norm(result, edge_scale[...]).reshape(step, keys, width)
    live = live_row[window, :][:, None, :] * live_key[...][None]
    edges_out[...] = (normed * live).astype(edges_out.dtype)


def finish(n_ka, hidden, pair, states, *rest):
    rows, keys, width = pair.shape
    frames = rest[1]
    step = 8
    count = states.shape[0]

    def whole(array):
        return pl.BlockSpec(
            array.shape, lambda i: (0,) * len(array.shape), pipeline_mode=pl.Buffered(1)
        )

    outs = (
        jax.ShapeDtypeStruct((rows, C_S), jnp.float32),
        jax.ShapeDtypeStruct(frames.shape, jnp.float32),
        jax.ShapeDtypeStruct(pair.shape, jnp.bfloat16),
    )
    return pl.pallas_call(
        functools.partial(finish_kernel, n_ka),
        grid=(rows // step,),
        out_shape=outs,
        in_specs=[
            pl.BlockSpec((step, keys, EH), lambda i: (i, 0, 0)),
            pl.BlockSpec((step, keys, width), lambda i: (i, 0, 0)),
        ]
        + [whole(array) for array in (states, *rest)],
        out_specs=(
            pl.BlockSpec((rows, C_S), lambda i: (0, 0)),
            pl.BlockSpec(frames.shape, lambda i: (0, 0)),
            pl.BlockSpec((step, keys, width), lambda i: (i, 0, 0)),
        ),
        scratch_shapes=[
            pltpu.VMEM((rows, EH), jnp.float32),
            pltpu.VMEM((keys, EH), jnp.float32),
            pltpu.VMEM((rows, width), jnp.float32),
            pltpu.VMEM((keys, width), jnp.float32),
            pltpu.VMEM((count, C_S), jnp.float32),
            pltpu.VMEM((count, 2 * C_S), jnp.bfloat16),
        ],
        compiler_params=pltpu.CompilerParams(vmem_limit_bytes=40 << 20),
    )(hidden, pair, states, *rest)


def on_device(
    node_states,
    frames,
    edge_states,
    chain_number,
    residue_index,
    padding_mask,
    query_weight,
    key_weight,
    value_weight,
    point_query,
    point_key,
    point_value,
    bias_weight,
    point_gamma,
    relpos_table,
    output_weight,
    attention_scales,
    layer_project,
    layer_output,
    layer_expand,
    layer_shrink,
    layer_scales,
    frame_weight,
    node_to_edge,
    edge_first,
    edge_second,
    edge_third,
    edge_biases,
    edge_scales,
):
    n_pb, n_ka = lax.axis_size("pb"), lax.axis_size("ka")
    mask = padding_mask[None]
    perm_qk, perm_v = by_component(QKP), by_component(VP)
    states, pair, hidden = attend(
        n_pb,
        n_ka,
        (
            node_states,
            frames,
            chain_number[None],
            residue_index[None],
            mask,
            point_query,
            point_key,
            point_value,
            bias_weight,
            point_gamma[None],
            relpos_table,
            attention_scales[None],
            jnp.asarray(perm_qk, jnp.bfloat16),
            jnp.asarray(perm_v, jnp.bfloat16),
            jnp.asarray(perm_v.T, jnp.bfloat16),
            edge_first,
        ),
        (edge_states, query_weight, key_weight, value_weight, output_weight),
    )
    return finish(
        n_ka,
        hidden,
        pair,
        states.reshape(-1, C_S),
        mask,
        frames,
        layer_project,
        layer_output,
        layer_expand,
        layer_shrink,
        layer_scales,
        frame_weight,
        node_to_edge,
        edge_second,
        edge_third,
        edge_biases,
        edge_scales[None],
    )


def solution(mesh):
    placed = [P()] * 29
    placed[:3] = [P("pb", None), P(None, "pb"), P("pb", "ka", None)]
    return jax.shard_map(
        on_device,
        mesh=mesh,
        in_specs=tuple(placed),
        out_specs=(P("pb", None), P(None, "pb"), P("pb", "ka", None)),
        check_vma=False,
    )
```

time: 107 us -> 70.2 us (0.66)
  matrix products: 23.9 us -> 0 us
  Pallas kernels: 62.3 us -> 44.8 us
  local copies, waits for them, and re-layouts: 11.2 us -> 23.7 us
  other arithmetic: 7.67 us -> 0 us
    dot_general x29 -> x0, matrix products: 23.9 us -> none  [the longest x3 6.27 us: place_points(): local = jnp.dot(features, spread, preferred_element_type=jnp.float32)]
    unnamed x58 -> x61, local copies, waits for them, and re-layouts: 2.47 us -> 23.7 us
    pallas_call x5 -> x2, Pallas kernels: 62.3 us -> 44.8 us  [the longest x1 29.2 us: attend(): pl.pallas_call(functools.partial(attend_kernel, n_pb, n_ka), out_shape=(j...]
    dynamic_slice x4 -> x0, local copies, waits for them, and re-layouts: 3.16 us -> none  [the longest x1 0.89 us: on_device(): chain_keys = lax.dynamic_slice_in_dim(chain_number, key_first, key_count, 0)]
    broadcast_in_dim x5 -> x0, local copies, waits for them, and re-layouts: 1.77 us -> none  [the longest x1 0.71 us: edge_transition(): jnp.broadcast_to(mask_keys.astype(jnp.float32)[:, None], (keys, width))]
    transpose x2 -> x0, local copies, waits for them, and re-layouts: 1.68 us -> none  [the longest x1 1.68 us: gather_rows(): return jnp.transpose(out, (1, 0, 2, 3)).reshape(-1, x.shape[-1])]
    convert_element_type x6 -> x0, other arithmetic: 1.66 us -> none  [the longest x1 0.82 us: on_device(): pair_rep = (edge_states.astype(jnp.float32) + relative).astype(jnp.bfloat16)]
    reduce_sum x4 -> x0, other arithmetic: 1.46 us -> none  [the longest x1 0.91 us: on_device(): factor = factor / jnp.sum(totals * factor, axis=0)]
where the time goes in v1:
time: 70.2 us; the launch traced here: 69.4 us
  Pallas kernels  44.8 us (64%)
  local copies, waits for them, and re-layouts  23.7 us (34%)
  between operations  0.83 us (1%)
    pallas_call x1, Pallas kernels, attend(): pl.pallas_call(functools.partial(attend_kernel, n_pb, n_ka), out_shape=(j...  29.2 us
    unnamed x61, local copies, waits for them, and re-layouts  23.7 us
    pallas_call x1, Pallas kernels, finish(): pl.pallas_call(functools.partial(finish_kernel, n_ka), grid=(rows // step...  15.7 us

profile of v1, /device:TPU:1, one launch (start us, length us, event | category | flops | bytes accessed | tf_op | source)
XLA Modules:
  0.0 69.4 jit_solution(10464016504039780580)
XLA Ops:
  0.6 0.8 %copy.38.bias_weight = bf16[128,8]{1,0:T(8,128)(2,1)S(1)} copy(bf16[128,8]{0,1:T(8,128)(2,1)} %param.44) | data formatting | bytes 4096 | tf_op args[12]
  1.4 1.0 %copy.35.point_query = bf16[256,192]{1,0:T(8,128)(2,1)S(1)} copy(bf16[256,192]{0,1:T(8,128)(2,1)} %param.41) | data formatting | bytes 196608 | tf_op args[9]
  2.4 1.0 %copy.36.point_key = bf16[256,192]{1,0:T(8,128)(2,1)S(1)} copy(bf16[256,192]{0,1:T(8,128)(2,1)} %param.42) | data formatting | bytes 196608 | tf_op args[10]
  3.4 0.8 %copy.39.frame_weight = f32[256,6]{1,0:T(8,128)S(1)} copy(f32[256,6]{0,1:T(8,128)} %param.54) | data formatting | bytes 12288 | tf_op args[22]
  4.3 1.1 %copy.37.point_value = bf16[256,288]{1,0:T(8,128)(2,1)S(1)} copy(bf16[256,288]{0,1:T(8,128)(2,1)} %param.43) | data formatting | bytes 294912 | tf_op args[11]
  5.3 0.0 copy-start.1
  5.4 1.6 %copy-done.1 = bf16[64,128,128]{2,1,0:T(8,128)(2,1)S(1)} copy-done((bf16[64,128,128]{2,1,0:T(8,128)(2,1)S(1)}, bf16[64,128,128]{2,1,0:T(8,128)(2,1)}, u32[]{:S(2)}) %copy-start.1) | copy-done | bytes 2097176
  6.9 1.5 %copy-done.2 = bf16[3456,256]{1,0:T(8,128)(2,1)S(1)} copy-done((bf16[3456,256]{1,0:T(8,128)(2,1)S(1)}, bf16[3456,256]{1,0:T(8,128)(2,1)}, u32[]{:S(2)}) %copy-start.2) | copy-done | bytes 1769496
  8.4 1.2 %copy-done.3 = bf16[256,2048]{1,0:T(8,128)(2,1)S(1)} copy-done((bf16[256,2048]{1,0:T(8,128)(2,1)S(1)}, bf16[256,2048]{1,0:T(8,128)(2,1)}, u32[]{:S(2)}) %copy-start.3) | copy-done | bytes 1048600
  9.6 1.2 %copy-done.4 = bf16[256,2048]{1,0:T(8,128)(2,1)S(1)} copy-done((bf16[256,2048]{1,0:T(8,128)(2,1)S(1)}, bf16[256,2048]{1,0:T(8,128)(2,1)}, u32[]{:S(2)}) %copy-start.4) | copy-done | bytes 1048600
  10.9 1.2 %copy-done.5 = bf16[256,2048]{1,0:T(8,128)(2,1)S(1)} copy-done((bf16[256,2048]{1,0:T(8,128)(2,1)S(1)}, bf16[256,2048]{1,0:T(8,128)(2,1)}, u32[]{:S(2)}) %copy-start.5) | copy-done | bytes 1048600
  12.1 1.0 %copy-done.9 = bf16[384,288]{1,0:T(8,128)(2,1)S(1)} copy-done((bf16[384,288]{1,0:T(8,128)(2,1)S(1)}, bf16[384,288]{1,0:T(8,128)(2,1)}, u32[]{:S(2)}) %copy-start.9) | copy-done | bytes 221208
  13.1 0.9 %copy-done.13 = bf16[288,384]{1,0:T(8,128)(2,1)S(1)} copy-done((bf16[288,384]{1,0:T(8,128)(2,1)S(1)}, bf16[288,384]{1,0:T(8,128)(2,1)}, u32[]{:S(2)}) %copy-start.13) | copy-done | bytes 221208
  14.0 0.9 %copy-done.14 = bf16[192,384]{1,0:T(8,128)(2,1)S(1)} copy-done((bf16[192,384]{1,0:T(8,128)(2,1)S(1)}, bf16[192,384]{1,0:T(8,128)(2,1)}, u32[]{:S(2)}) %copy-start.14) | copy-done | bytes 147480
  14.9 0.9 %copy-done.15 = bf16[128,384]{1,0:T(8,128)(2,1)S(1)} copy-done((bf16[128,384]{1,0:T(8,128)(2,1)S(1)}, bf16[128,384]{1,0:T(8,128)(2,1)}, u32[]{:S(2)}) %copy-start.15) | copy-done | bytes 98328
  15.8 0.8 %copy-done.17 = f32[64,256]{1,0:T(8,128)S(1)} copy-done((f32[64,256]{1,0:T(8,128)S(1)}, f32[64,256]{1,0:T(8,128)}, u32[]{:S(2)}) %copy-start.17) | copy-done | bytes 65560
  16.6 0.8 %copy-done.18 = f32[128,128]{1,0:T(8,128)S(1)} copy-done((f32[128,128]{1,0:T(8,128)S(1)}, f32[128,128]{1,0:T(8,128)}, u32[]{:S(2)}) %copy-start.18) | copy-done | bytes 65560
  17.5 0.7 %copy-done.19 = f32[12,64]{1,0:T(8,128)S(1)} copy-done((f32[12,64]{1,0:T(8,128)S(1)}, f32[12,64]{1,0:T(8,128)}, u32[]{:S(2)}) %copy-start.19) | copy-done | bytes 3096
  18.2 0.7 copy-done.20
  18.9 0.7 copy-done.23
  19.5 0.7 copy-done.24
  20.2 0.7 copy-done.25
  20.9 0.7 copy-done.26
  21.6 0.0 copy-start.11
  21.6 0.0 copy-start.12
  21.6 0.0 copy-start.16
  21.6 0.0 copy-start.21
  21.6 0.0 copy-start.22
  21.6 0.0 copy-start.27
  21.6 29.2 %shard_map.319 = (bf16[8,4,16,256]{3,2,1,0:T(8,128)(2,1)S(1)}, bf16[64,128,128]{2,1,0:T(8,128)(2,1)S(1)}, bf16[64,128,384]{2,1,0:T(8,128)(2,1)}) custom-call(f32[64,256]{1,0:T(8,128)S(1)} %copy-done.17, f32[12,64]{1,0:T(8,128)S(1)} %copy-done.19, s32[1,512]{1,0:T(1,128)S(1)} %bitcast.10, s32[1,512]{1,0:T(1,128)S(1)} %bitcast.11, s32[1,512]{1,0:T(1,128)S(1)} %bitcast.8, ...), custom_call_target="tpu_custom_call" | custom-call | tf_op jit(solution)/shard_map/pallas_call | solution.py:497
  50.9 2.8 %copy-done = bf16[64,128,384]{2,1,0:T(8,128)(2,1)S(1)} copy-done((bf16[64,128,384]{2,1,0:T(8,128)(2,1)S(1)}, bf16[64,128,384]{2,1,0:T(8,128)(2,1)}, u32[]{:S(2)}) %copy-start) | copy-done | bytes 6291480
  53.7 15.7 %shard_map.320 = (f32[64,256]{1,0:T(8,128)}, f32[12,64]{1,0:T(8,128)}, bf16[64,128,128]{2,1,0:T(8,128)(2,1)}) custom-call(bf16[64,128,384]{2,1,0:T(8,128)(2,1)S(1)} %copy-done, bf16[64,128,128]{2,1,0:T(8,128)(2,1)S(1)} %get-tuple-element.7.pair_ref, bf16[512,256]{1,0:T(8,128)(2,1)S(1)} %bitcast.7, s32[1,512]{1,0:T(1,128)S(1)} %bitcast.9, ...), custom_call_target="tpu_custom_call" | custom-call | tf_op jit(solution)/shard_map/pallas_call | solution.py:686
  (31 shorter events, 0.1 us)
Async XLA Ops:
  5.3 1.6 %copy-start.1 = (bf16[64,128,128]{2,1,0:T(8,128)(2,1)S(1)}, bf16[64,128,128]{2,1,0:T(8,128)(2,1)}, u32[]{:S(2)}) copy-start(bf16[64,128,128]{2,1,0:T(8,128)(2,1)} %edge_hbm.1) | copy-start | bytes 6291460
  6.9 1.5 %copy-start.2 = (bf16[3456,256]{1,0:T(8,128)(2,1)S(1)}, bf16[3456,256]{1,0:T(8,128)(2,1)}, u32[]{:S(2)}) copy-start(bf16[3456,256]{1,0:T(8,128)(2,1)} %ow_hbm.1) | copy-start | bytes 5308420
  8.4 1.2 %copy-start.3 = (bf16[256,2048]{1,0:T(8,128)(2,1)S(1)}, bf16[256,2048]{1,0:T(8,128)(2,1)}, u32[]{:S(2)}) copy-start(bf16[256,2048]{1,0:T(8,128)(2,1)} %wq_hbm.1) | copy-start | bytes 3145732
  9.6 1.2 %copy-start.4 = (bf16[256,2048]{1,0:T(8,128)(2,1)S(1)}, bf16[256,2048]{1,0:T(8,128)(2,1)}, u32[]{:S(2)}) copy-start(bf16[256,2048]{1,0:T(8,128)(2,1)} %wk_hbm.1) | copy-start | bytes 3145732
  10.9 1.2 %copy-start.5 = (bf16[256,2048]{1,0:T(8,128)(2,1)S(1)}, bf16[256,2048]{1,0:T(8,128)(2,1)}, u32[]{:S(2)}) copy-start(bf16[256,2048]{1,0:T(8,128)(2,1)} %wv_hbm.1) | copy-start | bytes 3145732
  12.1 1.0 %copy-start.9 = (bf16[384,288]{1,0:T(8,128)(2,1)S(1)}, bf16[384,288]{1,0:T(8,128)(2,1)}, u32[]{:S(2)}) copy-start(bf16[384,288]{1,0:T(8,128)(2,1)} %constant.8.clone.perm_vt) | copy-start | bytes 663556
  13.1 0.9 %copy-start.13 = (bf16[288,384]{1,0:T(8,128)(2,1)S(1)}, bf16[288,384]{1,0:T(8,128)(2,1)}, u32[]{:S(2)}) copy-start(bf16[288,384]{1,0:T(8,128)(2,1)} %constant.7.clone.perm_v) | copy-start | bytes 663556
  14.0 0.9 %copy-start.14 = (bf16[192,384]{1,0:T(8,128)(2,1)S(1)}, bf16[192,384]{1,0:T(8,128)(2,1)}, u32[]{:S(2)}) copy-start(bf16[192,384]{1,0:T(8,128)(2,1)} %constant.6.clone.perm_qk) | copy-start | bytes 442372
  14.9 0.9 %copy-start.15 = (bf16[128,384]{1,0:T(8,128)(2,1)S(1)}, bf16[128,384]{1,0:T(8,128)(2,1)}, u32[]{:S(2)}) copy-start(bf16[128,384]{1,0:T(8,128)(2,1)} %first.1) | copy-start | bytes 294916
  15.8 0.8 %copy-start.17 = (f32[64,256]{1,0:T(8,128)S(1)}, f32[64,256]{1,0:T(8,128)}, u32[]{:S(2)}) copy-start(f32[64,256]{1,0:T(8,128)} %node.1) | copy-start | bytes 196612
  16.6 0.8 %copy-start.18 = (f32[128,128]{1,0:T(8,128)S(1)}, f32[128,128]{1,0:T(8,128)}, u32[]{:S(2)}) copy-start(f32[128,128]{1,0:T(8,128)} %relpos.1) | copy-start | bytes 196612
  17.5 0.7 %copy-start.19 = (f32[12,64]{1,0:T(8,128)S(1)}, f32[12,64]{1,0:T(8,128)}, u32[]{:S(2)}) copy-start(f32[12,64]{1,0:T(8,128)} %frames.3) | copy-start | bytes 9220
  18.2 0.7 copy-start.20
  18.9 0.7 copy-start.23
  19.5 0.7 copy-start.24
  20.2 0.7 copy-start.25
  20.9 0.7 copy-start.26
  21.6 29.3 %copy-start.6 = (bf16[2,256,768]{2,1,0:T(8,128)(2,1)S(1)}, bf16[2,256,768]{2,1,0:T(8,128)(2,1)}, u32[]{:S(2)}) copy-start(bf16[2,256,768]{2,1,0:T(8,128)(2,1)} %project.1) | copy-start | bytes 2359300
  21.6 29.3 %copy-start.7 = (bf16[256,768]{1,0:T(8,128)(2,1)S(1)}, bf16[256,768]{1,0:T(8,128)(2,1)}, u32[]{:S(2)}) copy-start(bf16[256,768]{1,0:T(8,128)(2,1)} %to_edge.1) | copy-start | bytes 1179652
  21.6 29.3 %copy-start.8 = (bf16[384,384]{1,0:T(8,128)(2,1)S(1)}, bf16[384,384]{1,0:T(8,128)(2,1)}, u32[]{:S(2)}) copy-start(bf16[384,384]{1,0:T(8,128)(2,1)} %second.1) | copy-start | bytes 884740
  21.6 29.3 %copy-start.10 = (bf16[2,256,256]{2,1,0:T(8,128)(2,1)S(1)}, bf16[2,256,256]{2,1,0:T(8,128)(2,1)}, u32[]{:S(2)}) copy-start(bf16[2,256,256]{2,1,0:T(8,128)(2,1)} %output.1) | copy-start | bytes 786436
  21.6 29.3 %copy-start.11 = (bf16[2,256,256]{2,1,0:T(8,128)(2,1)S(1)}, bf16[2,256,256]{2,1,0:T(8,128)(2,1)}, u32[]{:S(2)}) copy-start(bf16[2,256,256]{2,1,0:T(8,128)(2,1)} %expand.1) | copy-start | bytes 786436
  21.6 29.3 %copy-start.12 = (bf16[2,256,256]{2,1,0:T(8,128)(2,1)S(1)}, bf16[2,256,256]{2,1,0:T(8,128)(2,1)}, u32[]{:S(2)}) copy-start(bf16[2,256,256]{2,1,0:T(8,128)(2,1)} %shrink.1) | copy-start | bytes 786436
  21.6 29.3 %copy-start.16 = (bf16[384,128]{1,0:T(8,128)(2,1)S(1)}, bf16[384,128]{1,0:T(8,128)(2,1)}, u32[]{:S(2)}) copy-start(bf16[384,128]{1,0:T(8,128)(2,1)} %third.1) | copy-start | bytes 294916
  21.6 29.3 %copy-start.21 = (f32[2,2,256]{2,1,0:T(2,128)S(1)}, f32[2,2,256]{2,1,0:T(2,128)}, u32[]{:S(2)}) copy-start(f32[2,2,256]{2,1,0:T(2,128)} %scales.1) | copy-start | bytes 12292
  21.6 29.3 %copy-start.22 = (f32[2,384]{1,0:T(2,128)S(1)}, f32[2,384]{1,0:T(2,128)}, u32[]{:S(2)}) copy-start(f32[2,384]{1,0:T(2,128)} %biases.1) | copy-start | bytes 9220
  21.6 29.3 %copy-start.27 = (f32[128]{0:T(128)S(1)}, f32[128]{0:T(128)}, u32[]{:S(2)}) copy-start(f32[128]{0:T(128)} %param.60) | copy-start | bytes 1540
  50.9 2.8 %copy-start = (bf16[64,128,384]{2,1,0:T(8,128)(2,1)S(1)}, bf16[64,128,384]{2,1,0:T(8,128)(2,1)}, u32[]{:S(2)}) copy-start(bf16[64,128,384]{2,1,0:T(8,128)(2,1)} %get-tuple-element.6.hidden_ref) | copy-start | bytes 18874372

commit v2 on v1

--- a/solution.py
+++ b/solution.py
@@ -24,9 +24,10 @@
 HIGHEST = lax.Precision.HIGHEST
 NEG_FILL = -1000000000.0
 CHAIN_STEP = 65536.0
+LOADS = 20
 MESH = pl.DeviceIdType.MESH
 VMEM = pl.BlockSpec(memory_space=pltpu.VMEM)
-ANY = pl.BlockSpec(memory_space=pl.ANY)
+HBM = pl.BlockSpec(memory_space=pltpu.HBM)
 
 
 def dot(a, b, **options):
@@ -83,64 +84,60 @@
 def attend_kernel(
     n_pb,
     n_ka,
-    node,
-    frames,
-    chain,
-    index,
-    mask,
-    point_query,
-    point_key,
-    point_value,
-    bias_weight,
-    gamma,
-    relpos,
-    scales,
-    perm_qk,
-    perm_v,
-    perm_vt,
-    first,
-    edge_hbm,
-    wq_hbm,
-    wk_hbm,
-    wv_hbm,
-    ow_hbm,
-    states_out,
-    pair_hbm,
-    hidden_hbm,
-    edge_s,
-    pair_s,
-    hidden_s,
-    wq,
-    wk,
-    wv,
-    ow,
-    x_send,
-    x_keys,
-    f_keys,
-    bias_s,
-    work_s,
-    stats_send,
-    stats_recv,
-    part_send,
-    part_recv,
-    columns_s,
-    node_s,
-    mine,
-    load_sem,
-    store_sem,
-    x_send_sem,
-    x_recv_sem,
-    f_send_sem,
-    f_recv_sem,
-    s_send_sem,
-    s_recv_sem,
-    p_send_sem,
-    p_recv_sem,
-    g_send_sem,
-    g_recv_sem,
-    h_send_sem,
-    h_recv_sem,
+    *refs,
 ):
+    sources, refs = refs[:LOADS], refs[LOADS:]
+    (states_out, pair_s, hidden_s), refs = refs[:3], refs[3:]
+    targets, refs = refs[:LOADS], refs[LOADS:]
+    (
+        node,
+        frames,
+        chain,
+        index,
+        mask,
+        relpos,
+        edge_s,
+        bias_rows_s,
+        first,
+        wq,
+        point_query,
+        point_key,
+        point_value,
+        perm_qk,
+        perm_v,
+        gamma,
+        wk,
+        wv,
+        scales,
+        ow,
+    ) = targets
+    (
+        x_send,
+        x_keys,
+        f_keys,
+        bias_s,
+        work_s,
+        stats_send,
+        stats_recv,
+        part_send,
+        part_recv,
+        columns_s,
+        node_s,
+        mine,
+        load_sem,
+            x_send_sem,
+        x_recv_sem,
+        f_send_sem,
+        f_recv_sem,
+        s_send_sem,
+        s_recv_sem,
+        p_send_sem,
+        p_recv_sem,
+        g_send_sem,
+        g_recv_sem,
+        h_send_sem,
+        h_recv_sem,
+    ) = refs
     rows, keys, channels = edge_s.shape
     count = chain.shape[1]
     part = rows // n_ka
@@ -155,12 +152,12 @@
         pl.semaphore_signal(barrier, inc=1, device_id=peer, device_id_type=MESH)
     loads = [
         pltpu.make_async_copy(source, target, load_sem.at[k])
-        for k, (source, target) in enumerate(
-            ((edge_hbm, edge_s), (wq_hbm, wq), (wk_hbm, wk), (wv_hbm, wv), (ow_hbm, ow))
-        )
+        for k, (source, target) in enumerate(zip(sources, targets))
     ]
     for load in loads:
         load.start()
+    for load in loads[:6]:
+        load.wait()
 
     x_send[...] = node[...].astype(jnp.bfloat16)
 
@@ -180,9 +177,9 @@
     low = (table - high.astype(jnp.float32)).astype(jnp.bfloat16)
     table = jnp.concatenate([high, low], axis=1)
     bin_lane = iota((keys, RELBINS), 1).astype(jnp.float32)
-    eye = (iota((channels, channels), 0) == iota((channels, channels), 1)).astype(jnp.bfloat16)
-    bias_rows = contract(bias_weight[...], eye, 0, 0).astype(jnp.bfloat16)
-    loads[0].wait()
+    for load in loads[6:8]:
+        load.wait()
+    bias_rows = bias_rows_s[...]
 
     def pair_rows(start, size):
         onehot = jnp.concatenate(
@@ -243,20 +240,19 @@
 
     for start in late:
         pair_rows(start, group)
-    pair_store = pltpu.make_async_copy(pair_s, pair_hbm, store_sem.at[0])
-    pair_store.start()
 
     own_columns = frame_columns(frames[...])
     for a in range(n_ka):
         columns_s[a] = own_columns[a * part : (a + 1) * part]
         node_s[a] = node[a * part : (a + 1) * part, :]
     own = x_send[...]
-    loads[1].wait()
+    for load in loads[8:16]:
+        load.wait()
     queries = dot(own, wq[...]).astype(jnp.bfloat16)
-    spread = dot(point_query[...], perm_qk[...]).astype(jnp.bfloat16)
-    query_places = place(dot(own, spread), own_columns)
-    spread_key = dot(point_key[...], perm_qk[...]).astype(jnp.bfloat16)
-    spread_value = dot(point_value[...], perm_v[...]).astype(jnp.bfloat16)
+    spread = dot(perm_qk[...], point_query[...]).astype(jnp.bfloat16)
+    query_places = place(contract(own, spread, 1, 1), own_columns)
+    spread_key = dot(perm_qk[...], point_key[...]).astype(jnp.bfloat16)
+    spread_value = dot(perm_v[...], point_value[...]).astype(jnp.bfloat16)
     heads_qk = head_of_lane(QKP)
     by_head = (query_places[:, None, :] * heads_qk[None]).reshape(rows * HEADS, 3 * LANES)
     query_square = jnp.sum(by_head * by_head, axis=-1, keepdims=True)
@@ -284,10 +280,10 @@
 
     key_rows = jnp.concatenate([x_keys[slot] for slot in range(per)], axis=0)
     key_columns = jnp.concatenate([frame_columns(f_keys[slot]) for slot in range(per)], axis=0)
-    key_places = place(dot(key_rows, spread_key), key_columns)
+    key_places = place(contract(key_rows, spread_key, 1, 1), key_columns)
     cross = contract(by_head, key_places, 1, 1, precision=HIGHEST)
     key_square = contract(heads_qk, key_places * key_places, 1, 1, precision=HIGHEST)
-    loads[2].wait()
+    loads[16].wait()
     key_vectors = dot(key_rows, wk[...]).astype(jnp.bfloat16)
     for head in range(HEADS):
         window = slice(head * HD, (head + 1) * HD)
@@ -329,7 +325,7 @@
 
     work_s[...] = weights.reshape(rows * HEADS, keys)
     rounded = weights.astype(jnp.bfloat16)
-    loads[3].wait()
+    loads[17].wait()
     value_vectors = dot(key_rows, wv[...]).astype(jnp.bfloat16)
     scalar = [
         dot(
@@ -339,7 +335,7 @@
         for head in range(HEADS)
     ]
     pair_out = jnp.stack([dot(rounded[i], pair_s[i]) for i in range(rows)], axis=0)
-    value_places = place(dot(key_rows, spread_value), key_columns)
+    value_places = place(contract(key_rows, spread_value, 1, 1), key_columns)
     heads_v = head_of_lane(VP)
     points = dot(weights.reshape(rows * HEADS, keys), value_places, precision=HIGHEST)
 
@@ -357,7 +353,8 @@
     factor = jnp.sum(jnp.where(at_lane, share[None], 0.0), axis=-1, keepdims=True)
     bias_s[...] = jnp.broadcast_to(factor, (rows, HEADS, keys)).reshape(rows * HEADS, keys)
     work_s[...] = (pair_out * factor).reshape(rows * HEADS, channels)
-    loads[4].wait()
+    for load in loads[18:]:
+        load.wait()
     features = []
     for head in range(HEADS):
         scale = bias_s[pl.ds(head, rows, stride=HEADS), :]
@@ -390,18 +387,12 @@
         pair = pair_s[start : start + group].reshape(group * keys, channels)
         values = dot(pair, first[...]).astype(jnp.bfloat16)
         hidden_s[start : start + group] = values.reshape(group, keys, EH)
-        store = pltpu.make_async_copy(
-            hidden_s.at[pl.ds(start, group)],
-            hidden_hbm.at[pl.ds(start, group)],
-            store_sem.at[1 + start // group],
-        )
-        store.start()
-        return store
 
     third = -(-len(starts) // 3)
-    stores = [hidden_rows(start) for start in starts[:third]]
+    for start in starts[:third]:
+        hidden_rows(start)
     value_base = HEADS * (HD + C_Z)
-    point_weight = dot(perm_vt[...], ow[value_base : value_base + HEADS * 3 * VP, :]).astype(
+    point_weight = dot(perm_v[...], ow[value_base : value_base + HEADS * 3 * VP, :]).astype(
         jnp.bfloat16
     )
     for copy in parts:
@@ -441,7 +432,8 @@
     ]
     for copy in gathers:
         copy.start()
-    stores += [hidden_rows(start) for start in starts[third : 2 * third]]
+    for start in starts[third : 2 * third]:
+        hidden_rows(start)
     for copy in gathers:
         copy.wait()
     spreads = [
@@ -457,7 +449,8 @@
     ]
     for copy in spreads:
         copy.start()
-    stores += [hidden_rows(start) for start in starts[2 * third :]]
+    for start in starts[2 * third :]:
+        hidden_rows(start)
     for slot in range(per):
 
         @pl.when(row == col * per + slot)
@@ -482,13 +475,10 @@
 
     for copy in spreads:
         copy.wait()
-    pair_store.wait()
-    for store in stores:
-        store.wait()
-
-
-def attend(n_pb, n_ka, small, large):
-    node, frames, edge = small[0], small[1], large[0]
+
+
+def attend(n_pb, n_ka, *operands):
+    frames, edge = operands[1], operands[6]
     rows, keys, channels = edge.shape
     part, per = rows // n_ka, n_pb // n_ka
     lanes = -(-rows // LANES) * LANES
@@ -501,13 +491,10 @@
             jax.ShapeDtypeStruct(edge.shape, bf16),
             jax.ShapeDtypeStruct((rows, keys, EH), bf16),
         ),
-        in_specs=[VMEM] * len(small) + [ANY] * len(large),
-        out_specs=(VMEM, ANY, ANY),
+        in_specs=[HBM] * len(operands),
+        out_specs=(VMEM,) * 3,
         scratch_shapes=[
-            pltpu.VMEM(edge.shape, bf16),
-            pltpu.VMEM(edge.shape, bf16),
-            pltpu.VMEM((rows, keys, EH), bf16),
-            *[pltpu.VMEM(array.shape, bf16) for array in large[1:]],
+            *[pltpu.VMEM(array.shape, array.dtype) for array in operands],
             pltpu.VMEM((rows, C_S), bf16),
             pltpu.VMEM((per, rows, C_S), bf16),
             pltpu.VMEM((per,) + frames.shape, f32),
@@ -520,8 +507,7 @@
             pltpu.VMEM((n_ka, part, LANES), f32),
             pltpu.VMEM((n_ka, part, C_S), f32),
             pltpu.VMEM((part, C_S), bf16),
-            dma((len(large),)),
-            dma((1 + rows // 8,)),
+            dma((len(operands),)),
             dma((n_pb - 1,)),
             dma((per,)),
             dma((n_pb - 1,)),
@@ -536,9 +522,9 @@
             dma((n_ka - 1,)),
         ],
         compiler_params=pltpu.CompilerParams(
-            collective_id=0, has_side_effects=True, vmem_limit_bytes=40 << 20
+            collective_id=0, has_side_effects=True, vmem_limit_bytes=28 << 20
         ),
-    )(*small, *large)
+    )(*[pltpu.with_memory_space_constraint(array, pltpu.HBM) for array in operands])
 
 
 def encoder_rows(states, key_value, fill, project, output, expand, shrink, scales):
@@ -560,7 +546,7 @@
 
 
 def update_frames(states, frames, frame_weight):
-    update = contract(frame_weight, states, 0, 1, precision=HIGHEST)
+    update = contract(frame_weight, states, 1, 1, precision=HIGHEST)
     x, y, z = update[0:1], update[1:2], update[2:3]
     length = jnp.sqrt(1.0 + x * x + y * y + z * z)
     w, x, y, z = 1.0 / length, x / length, y / length, z / length
@@ -705,7 +691,7 @@
             pltpu.VMEM((count, C_S), jnp.float32),
             pltpu.VMEM((count, 2 * C_S), jnp.bfloat16),
         ],
-        compiler_params=pltpu.CompilerParams(vmem_limit_bytes=40 << 20),
+        compiler_params=pltpu.CompilerParams(vmem_limit_bytes=28 << 20),
     )(hidden, pair, states, *rest)
 
 
@@ -742,29 +728,30 @@
 ):
     n_pb, n_ka = lax.axis_size("pb"), lax.axis_size("ka")
     mask = padding_mask[None]
-    perm_qk, perm_v = by_component(QKP), by_component(VP)
+    perm_qk, perm_v = (jnp.asarray(by_component(k).T, jnp.bfloat16) for k in (QKP, VP))
     states, pair, hidden = attend(
         n_pb,
         n_ka,
-        (
-            node_states,
-            frames,
-            chain_number[None],
-            residue_index[None],
-            mask,
-            point_query,
-            point_key,
-            point_value,
-            bias_weight,
-            point_gamma[None],
-            relpos_table,
-            attention_scales[None],
-            jnp.asarray(perm_qk, jnp.bfloat16),
-            jnp.asarray(perm_v, jnp.bfloat16),
-            jnp.asarray(perm_v.T, jnp.bfloat16),
-            edge_first,
-        ),
-        (edge_states, query_weight, key_weight, value_weight, output_weight),
+        node_states,
+        frames,
+        chain_number[None],
+        residue_index[None],
+        mask,
+        relpos_table,
+        edge_states,
+        jnp.transpose(bias_weight),
+        edge_first,
+        query_weight,
+        jnp.transpose(point_query),
+        jnp.transpose(point_key),
+        jnp.transpose(point_value),
+        perm_qk,
+        perm_v,
+        point_gamma[None],
+        key_weight,
+        value_weight,
+        attention_scales[None],
+        output_weight,
     )
     return finish(
         n_ka,
@@ -778,7 +765,7 @@
         layer_expand,
         layer_shrink,
         layer_scales,
-        frame_weight,
+        jnp.transpose(frame_weight),
         node_to_edge,
         edge_second,
         edge_third,

time: 70.2 us -> 46.3 us (0.66); the launches traced: 69.4 us -> 46.2 us
  local copies, waits for them, and re-layouts: 23.7 us -> 0.05 us
    unnamed x61 -> x26, local copies, waits for them, and re-layouts: 23.7 us -> 0.05 us
where the time goes in v2:
time: 46.3 us; the launch traced here: 46.2 us
  Pallas kernels  45.3 us (98%)
  between operations  0.85 us (2%)
    pallas_call x1, Pallas kernels, attend(): pl.pallas_call(functools.partial(attend_kernel, n_pb, n_ka), out_shape=(j...  29.4 us
    pallas_call x1, Pallas kernels, finish(): pl.pallas_call(functools.partial(finish_kernel, n_ka), grid=(rows // step...  15.9 us

profile of v2, /device:TPU:1, one launch (start us, length us, event | category | flops | bytes accessed | tf_op | source)
XLA Modules:
  0.0 46.2 jit_solution(2906197196663424922)
XLA Ops:
  0.6 0.0 copy-start
  0.6 0.0 copy-start.1
  0.7 0.0 copy-start.2
  0.7 0.0 copy-start.3
  0.7 0.0 copy-start.4
  0.7 0.0 copy-start.5
  0.7 0.0 copy-start.6
  0.7 0.0 copy-start.7
  0.7 0.0 copy-start.8
  0.7 0.0 copy-start.9
  0.7 0.0 copy-start.10
  0.7 0.0 copy-start.11
  0.8 0.0 copy-start.12
  0.8 29.4 %shard_map.310 = (bf16[8,4,16,256]{3,2,1,0:T(8,128)(2,1)S(1)}, bf16[64,128,128]{2,1,0:T(8,128)(2,1)S(1)}, bf16[64,128,384]{2,1,0:T(8,128)(2,1)S(1)}) custom-call(f32[64,256]{1,0:T(8,128)} %refs_0_.1, f32[12,64]{1,0:T(8,128)} %frames.1, s32[1,512]{1,0:T(1,128)} %bitcast.20, s32[1,512]{1,0:T(1,128)} %bitcast.21, s32[1,512]{1,0:T(1,128)} %bitcast.14, ...), custom_call_target="tpu_custom_call" | custom-call | tf_op jit(solution)/shard_map/pallas_call | solution.py:487
  30.2 0.0 copy-done
  30.2 0.0 copy-done.1
  30.2 0.0 copy-done.2
  30.2 0.0 copy-done.3
  30.2 0.0 copy-done.4
  30.2 0.0 copy-done.5
  30.2 0.0 copy-done.6
  30.2 0.0 copy-done.7
  30.3 0.0 copy-done.8
  30.3 0.0 copy-done.9
  30.3 0.0 copy-done.10
  30.3 0.0 copy-done.11
  30.3 0.0 copy-done.12
  30.3 15.9 %shard_map.311 = (f32[64,256]{1,0:T(8,128)}, f32[12,64]{1,0:T(8,128)}, bf16[64,128,128]{2,1,0:T(8,128)(2,1)}) custom-call(bf16[64,128,384]{2,1,0:T(8,128)(2,1)S(1)} %get-tuple-element.6.hidden_ref, bf16[64,128,128]{2,1,0:T(8,128)(2,1)S(1)} %get-tuple-element.7.pair_ref, bf16[512,256]{1,0:T(8,128)(2,1)S(1)} %bitcast.12, s32[1,512]{1,0:T(1,128)S(1)} %bitcast.15, ...), custom_call_target="tpu_custom_call" | custom-call | tf_op jit(solution)/shard_map/pallas_call | solution.py:672
Async XLA Ops:
  0.6 29.5 %copy-start = (bf16[2,256,768]{2,1,0:T(8,128)(2,1)S(1)}, bf16[2,256,768]{2,1,0:T(8,128)(2,1)}, u32[]{:S(2)}) copy-start(bf16[2,256,768]{2,1,0:T(8,128)(2,1)} %project.1) | copy-start | bytes 2359300
  0.6 29.5 %copy-start.1 = (bf16[256,768]{1,0:T(8,128)(2,1)S(1)}, bf16[256,768]{1,0:T(8,128)(2,1)}, u32[]{:S(2)}) copy-start(bf16[256,768]{1,0:T(8,128)(2,1)} %to_edge.1) | copy-start | bytes 1179652
  0.7 29.5 %copy-start.2 = (bf16[384,384]{1,0:T(8,128)(2,1)S(1)}, bf16[384,384]{1,0:T(8,128)(2,1)}, u32[]{:S(2)}) copy-start(bf16[384,384]{1,0:T(8,128)(2,1)} %second.1) | copy-start | bytes 884740
  0.7 29.5 %copy-start.3 = (bf16[2,256,256]{2,1,0:T(8,128)(2,1)S(1)}, bf16[2,256,256]{2,1,0:T(8,128)(2,1)}, u32[]{:S(2)}) copy-start(bf16[2,256,256]{2,1,0:T(8,128)(2,1)} %output.1) | copy-start | bytes 786436
  0.7 29.5 %copy-start.4 = (bf16[2,256,256]{2,1,0:T(8,128)(2,1)S(1)}, bf16[2,256,256]{2,1,0:T(8,128)(2,1)}, u32[]{:S(2)}) copy-start(bf16[2,256,256]{2,1,0:T(8,128)(2,1)} %expand.1) | copy-start | bytes 786436
  0.7 29.5 %copy-start.5 = (bf16[2,256,256]{2,1,0:T(8,128)(2,1)S(1)}, bf16[2,256,256]{2,1,0:T(8,128)(2,1)}, u32[]{:S(2)}) copy-start(bf16[2,256,256]{2,1,0:T(8,128)(2,1)} %shrink.1) | copy-start | bytes 786436
  0.7 29.5 %copy-start.6 = (bf16[384,128]{1,0:T(8,128)(2,1)S(1)}, bf16[384,128]{1,0:T(8,128)(2,1)}, u32[]{:S(2)}) copy-start(bf16[384,128]{1,0:T(8,128)(2,1)} %third.1) | copy-start | bytes 294916
  0.7 29.5 %copy-start.7 = (f32[12,64]{1,0:T(8,128)S(1)}, f32[12,64]{1,0:T(8,128)}, u32[]{:S(2)}) copy-start(f32[12,64]{1,0:T(8,128)} %frames.1) | copy-start | bytes 9220
  0.7 29.5 %copy-start.8 = (f32[256,6]{0,1:T(8,128)S(1)}, f32[256,6]{0,1:T(8,128)}, u32[]{:S(2)}) copy-start(f32[256,6]{0,1:T(8,128)} %param.53) | copy-start | bytes 18436
  0.7 29.5 %copy-start.9 = (s32[512]{0:T(512)S(1)}, s32[512]{0:T(512)}, u32[]{:S(2)}) copy-start(s32[512]{0:T(512)} %param.36) | copy-start | bytes 6148
  0.7 29.5 %copy-start.10 = (f32[2,2,256]{2,1,0:T(2,128)S(1)}, f32[2,2,256]{2,1,0:T(2,128)}, u32[]{:S(2)}) copy-start(f32[2,2,256]{2,1,0:T(2,128)} %scales.1) | copy-start | bytes 12292
  0.7 29.5 %copy-start.11 = (f32[2,384]{1,0:T(2,128)S(1)}, f32[2,384]{1,0:T(2,128)}, u32[]{:S(2)}) copy-start(f32[2,384]{1,0:T(2,128)} %biases.1) | copy-start | bytes 9220
  0.8 29.5 %copy-start.12 = (f32[128]{0:T(128)S(1)}, f32[128]{0:T(128)}, u32[]{:S(2)}) copy-start(f32[128]{0:T(128)} %param.59) | copy-start | bytes 1540

commit v3 on v2

--- a/solution.py
+++ b/solution.py
@@ -113,6 +113,7 @@
     ) = targets
     (
         x_send,
+        f_send,
         x_keys,
         f_keys,
         bias_s,
@@ -160,6 +161,7 @@
         load.wait()
 
     x_send[...] = node[...].astype(jnp.bfloat16)
+    f_send[...] = frames[...].astype(jnp.bfloat16)
 
     code = chain[...].astype(jnp.float32) * CHAIN_STEP + index[...].astype(jnp.float32)
     code = jnp.broadcast_to(code, (8, count))
@@ -201,8 +203,8 @@
 
     group = 8
     starts = list(range(0, rows, group))
-    early = starts[: len(starts) // 2]
-    late = starts[len(starts) // 2 :]
+    early = starts[: len(starts) // 4]
+    late = starts[len(starts) // 4 :]
     for start in early:
         pair_rows(start, group)
 
@@ -225,7 +227,7 @@
                 )
                 copies.append(
                     pltpu.make_async_remote_copy(
-                        src_ref=frames,
+                        src_ref=f_send,
                         dst_ref=f_keys.at[slot],
                         send_sem=f_send_sem.at[d],
                         recv_sem=f_recv_sem.at[slot],
@@ -236,7 +238,7 @@
             for copy in copies:
                 copy.start()
             x_keys[slot] = x_send[...]
-            f_keys[slot] = frames[...]
+            f_keys[slot] = f_send[...]
 
     for start in late:
         pair_rows(start, group)
@@ -270,7 +272,7 @@
                 device_id_type=MESH,
             ).wait_recv()
             pltpu.make_async_remote_copy(
-                src_ref=frames,
+                src_ref=f_send,
                 dst_ref=f_keys.at[slot],
                 send_sem=f_send_sem.at[0],
                 recv_sem=f_recv_sem.at[slot],
@@ -279,7 +281,7 @@
             ).wait_recv()
 
     key_rows = jnp.concatenate([x_keys[slot] for slot in range(per)], axis=0)
-    key_columns = jnp.concatenate([frame_columns(f_keys[slot]) for slot in range(per)], axis=0)
+    key_columns = jnp.concatenate([frame_columns(f_keys[slot].astype(jnp.float32)) for slot in range(per)], axis=0)
     key_places = place(contract(key_rows, spread_key, 1, 1), key_columns)
     cross = contract(by_head, key_places, 1, 1, precision=HIGHEST)
     key_square = contract(heads_qk, key_places * key_places, 1, 1, precision=HIGHEST)
@@ -432,25 +434,32 @@
     ]
     for copy in gathers:
         copy.start()
-    for start in starts[third : 2 * third]:
+
+    def forward(distance):
+        source = lax.rem(row + n_pb - distance, n_pb)
+        copies = [
+            pltpu.make_async_remote_copy(
+                src_ref=states_out.at[source, col] if distance else mine,
+                dst_ref=states_out.at[source, col],
+                send_sem=h_send_sem.at[distance, d],
+                recv_sem=h_recv_sem.at[distance, d],
+                device_id=peer,
+                device_id_type=MESH,
+            )
+            for d, peer in enumerate(along_ka)
+        ]
+        for copy in copies:
+            copy.start()
+        return copies
+
+    spreads = forward(0)
+    for start in starts[third:]:
         hidden_rows(start)
+    for distance in sorted(range(1, n_pb), key=lambda d: min(d, n_pb - d)):
+        gathers[distance - 1].wait_recv()
+        spreads += forward(distance)
     for copy in gathers:
-        copy.wait()
-    spreads = [
-        pltpu.make_async_remote_copy(
-            src_ref=states_out.at[:, col],
-            dst_ref=states_out.at[:, col],
-            send_sem=h_send_sem.at[d],
-            recv_sem=h_recv_sem.at[d],
-            device_id=peer,
-            device_id_type=MESH,
-        )
-        for d, peer in enumerate(along_ka)
-    ]
-    for copy in spreads:
-        copy.start()
-    for start in starts[2 * third :]:
-        hidden_rows(start)
+        copy.wait_send()
     for slot in range(per):
 
         @pl.when(row == col * per + slot)
@@ -465,7 +474,7 @@
                     device_id_type=MESH,
                 ).wait_send()
                 pltpu.make_async_remote_copy(
-                    src_ref=frames,
+                    src_ref=f_send,
                     dst_ref=f_keys.at[slot],
                     send_sem=f_send_sem.at[d],
                     recv_sem=f_recv_sem.at[slot],
@@ -496,8 +505,9 @@
         scratch_shapes=[
             *[pltpu.VMEM(array.shape, array.dtype) for array in operands],
             pltpu.VMEM((rows, C_S), bf16),
+            pltpu.VMEM(frames.shape, bf16),
             pltpu.VMEM((per, rows, C_S), bf16),
-            pltpu.VMEM((per,) + frames.shape, f32),
+            pltpu.VMEM((per,) + frames.shape, bf16),
             pltpu.VMEM((rows * HEADS, keys), f32),
             pltpu.VMEM((rows * HEADS, keys), f32),
             pltpu.VMEM((2, HEADS, lanes), f32),
@@ -518,8 +528,8 @@
             dma((n_ka - 1,)),
             dma((n_pb - 1,)),
             dma((n_pb - 1,)),
-            dma((n_ka - 1,)),
-            dma((n_ka - 1,)),
+            dma((n_pb, n_ka - 1)),
+            dma((n_pb, n_ka - 1)),
         ],
         compiler_params=pltpu.CompilerParams(
             collective_id=0, has_side_effects=True, vmem_limit_bytes=28 << 20
@@ -527,20 +537,26 @@
     )(*[pltpu.with_memory_space_constraint(array, pltpu.HBM) for array in operands])
 
 
-def encoder_rows(states, key_value, fill, project, output, expand, shrink, scales):
+def encoder_rows(states, keys, values, fill, project, output, expand, shrink, scales):
     queries = dot(states.astype(jnp.bfloat16), project[:, :C_S]).astype(
         jnp.bfloat16
     ) * jnp.asarray(1.0 / math.sqrt(TF_HD), jnp.bfloat16)
     owner = iota((1, C_S), 1) // TF_HD
-    context = jnp.zeros(states.shape, jnp.float32)
-    for head in range(C_S // TF_HD):
-        only = jnp.where(owner == head, 1.0, 0.0)
-        scores = contract(queries * only.astype(jnp.bfloat16), key_value[:, :C_S], 1, 1) + fill
-        weights = jnp.exp(scores - jnp.max(scores, axis=-1, keepdims=True))
-        inverse = 1.0 / jnp.sum(weights, axis=-1, keepdims=True)
-        mixed = dot(weights.astype(jnp.bfloat16), key_value[:, C_S:])
-        context = context + mixed * (inverse * only)
-    middle = layer_norm(states + dot(context.astype(jnp.bfloat16), output), scales[0:1])
+    context = []
+    for half in range(C_S // LANES):
+        mixed = None
+        for head in range(half * LANES // TF_HD, (half + 1) * LANES // TF_HD):
+            only = jnp.where(owner == head, 1.0, 0.0).astype(jnp.bfloat16)
+            scores = contract(queries * only, keys, 1, 1) + fill
+            weights = jnp.exp(scores - jnp.max(scores, axis=-1, keepdims=True))
+            sums = dot(weights.astype(jnp.bfloat16), values[head])
+            totals = sums[:, (1 - half) * LANES : (2 - half) * LANES]
+            sums = sums[:, half * LANES : (half + 1) * LANES] / totals
+            mine = owner[:, half * LANES : (half + 1) * LANES] == head
+            mixed = sums if mixed is None else jnp.where(mine, sums, mixed)
+        context.append(mixed.astype(jnp.bfloat16))
+    context = jnp.concatenate(context, axis=1)
+    middle = layer_norm(states + dot(context, output), scales[0:1])
     hidden = jnp.maximum(dot(middle.astype(jnp.bfloat16), expand), 0.0).astype(jnp.bfloat16)
     return layer_norm(middle + dot(hidden, shrink), scales[1:2])
 
@@ -592,7 +608,10 @@
     live_row,
     live_key,
     states_s,
-    key_value,
+    enc_keys,
+    enc_values,
+    second_tail,
+    third_tail,
 ):
     step, keys, width = pair_ref.shape
     rows = node_out.shape[0]
@@ -611,10 +630,19 @@
         live_row[...] = jnp.broadcast_to(contract(at_row, live, 1, 1)[:, 0:1], live_row.shape)
         live_key[...] = jnp.broadcast_to(contract(at_key, live, 1, 1)[:, 0:1], live_key.shape)
 
+        def attended(states, layer):
+            both = dot(states.astype(jnp.bfloat16), project[layer][:, C_S:]).astype(jnp.bfloat16)
+            enc_keys[...] = both[:, :C_S]
+            owner = iota((1, C_S), 1) // TF_HD
+            for head in range(C_S // TF_HD):
+                values = jnp.where(owner == head, both[:, C_S:].astype(jnp.float32), 1.0)
+                enc_values[head] = values.astype(jnp.bfloat16)
+
         def apply(states, layer):
             return encoder_rows(
                 states,
-                key_value[...],
+                enc_keys[...],
+                enc_values,
                 fill,
                 project[layer],
                 output[layer],
@@ -623,14 +651,12 @@
                 scales[layer],
             )
 
-        key_value[...] = dot(states_ref[...], project[0][:, C_S:]).astype(jnp.bfloat16)
-        chunk = math.gcd(count, 256)
+        attended(states_ref[...], 0)
+        chunk = math.gcd(count, 512)
         for start in range(0, count, chunk):
             window = slice(start, start + chunk)
             states_s[window, :] = apply(states_ref[window, :].astype(jnp.float32), 0)
-        key_value[...] = dot(states_s[...].astype(jnp.bfloat16), project[1][:, C_S:]).astype(
-            jnp.bfloat16
-        )
+        attended(states_s[...], 1)
         both = jnp.concatenate(
             [states_s[pl.ds(row_first, rows), :], states_s[pl.ds(key_first, keys), :]], axis=0
         )
@@ -638,6 +664,19 @@
         node_out[...] = final[:rows]
         row_part[...] = dot(final[:rows].astype(jnp.bfloat16), to_edge[:, :EH])
         key_part[...] = dot(final[rows:].astype(jnp.bfloat16), to_edge[:, EH:]) + biases[0:1]
+        wide = EH - LANES
+        zeros = jnp.zeros((LANES, LANES), jnp.bfloat16)
+        for target, block in (
+            (second_tail, second[wide:, wide:]),
+            (third_tail, third[wide:, :]),
+        ):
+            target[...] = jnp.concatenate(
+                [
+                    jnp.concatenate([block, zeros], axis=1),
+                    jnp.concatenate([zeros, block], axis=1),
+                ],
+                axis=0,
+            )
         frames_out[...] = update_frames(final[:rows], frames[...], frame_weight[...])
 
     window = pl.ds(pl.multiple_of(turn * step, step), step)
@@ -645,9 +684,19 @@
     hidden = hidden_ref[...].astype(jnp.float32)
     hidden = hidden + row_part[window, :][:, None, :] + key_part[...][None]
     hidden = jnp.maximum(hidden, 0.0).astype(jnp.bfloat16).reshape(step * keys, -1)
-    middle = dot(hidden, second[...]) + biases[1:2]
+    wide = EH - LANES
+
+    def tail(values, weights):
+        half = values.shape[0] // 2
+        both = jnp.concatenate([values[:half], values[half:]], axis=1)
+        both = dot(both, weights)
+        return jnp.concatenate([both[:, :LANES], both[:, LANES:]], axis=0)
+
+    middle = dot(hidden, second[:, :wide]) + biases[1:2, :wide]
     middle = jnp.maximum(middle, 0.0).astype(jnp.bfloat16)
-    result = pair.astype(jnp.float32) + dot(middle, third[...])
+    rest = dot(hidden[:, :wide], second[:wide, wide:]) + tail(hidden[:, wide:], second_tail[...])
+    rest = jnp.maximum(rest + biases[1:2, wide:], 0.0).astype(jnp.bfloat16)
+    result = pair.astype(jnp.float32) + dot(middle, third[:wide, :]) + tail(rest, third_tail[...])
     normed = layer_norm(result, edge_scale[...]).reshape(step, keys, width)
     live = live_row[window, :][:, None, :] * live_key[...][None]
     edges_out[...] = (normed * live).astype(edges_out.dtype)
@@ -656,7 +705,7 @@
 def finish(n_ka, hidden, pair, states, *rest):
     rows, keys, width = pair.shape
     frames = rest[1]
-    step = 8
+    step = math.gcd(rows, 16)
     count = states.shape[0]
 
     def whole(array):
@@ -689,7 +738,10 @@
             pltpu.VMEM((rows, width), jnp.float32),
             pltpu.VMEM((keys, width), jnp.float32),
             pltpu.VMEM((count, C_S), jnp.float32),
-            pltpu.VMEM((count, 2 * C_S), jnp.bfloat16),
+            pltpu.VMEM((count, C_S), jnp.bfloat16),
+            pltpu.VMEM((C_S // TF_HD, count, C_S), jnp.bfloat16),
+            pltpu.VMEM((2 * LANES, 2 * LANES), jnp.bfloat16),
+            pltpu.VMEM((2 * LANES, 2 * LANES), jnp.bfloat16),
         ],
         compiler_params=pltpu.CompilerParams(vmem_limit_bytes=28 << 20),
     )(hidden, pair, states, *rest)

time: 46.3 us -> 45 us (0.972)
  Pallas kernels: 45.3 us -> 43.6 us
    pallas_call x1, Pallas kernels: 15.9 us -> 14.3 us  [finish(): pl.pallas_call(functools.partial(finish_kernel, n_ka), grid=(rows // step...]
where the time goes in v3:
time: 45 us; the launch traced here: 44.5 us
  Pallas kernels  43.6 us (97%)
  between operations  0.85 us (2%)
    pallas_call x1, Pallas kernels, attend(): pl.pallas_call(functools.partial(attend_kernel, n_pb, n_ka), out_shape=(j...  29.3 us
    pallas_call x1, Pallas kernels, finish(): pl.pallas_call(functools.partial(finish_kernel, n_ka), grid=(rows // step...  14.3 us

profile of v3, /device:TPU:1, one launch (start us, length us, event | category | flops | bytes accessed | tf_op | source)
XLA Modules:
  0.0 44.5 jit_solution(8809572867520898986)
XLA Ops:
  0.6 0.0 copy-start
  0.6 0.0 copy-start.1
  0.7 0.0 copy-start.2
  0.7 0.0 copy-start.3
  0.7 0.0 copy-start.4
  0.7 0.0 copy-start.5
  0.7 0.0 copy-start.6
  0.7 0.0 copy-start.7
  0.7 0.0 copy-start.8
  0.7 0.0 copy-start.9
  0.7 0.0 copy-start.10
  0.7 0.0 copy-start.11
  0.8 0.0 copy-start.12
  0.8 29.3 %shard_map.310 = (bf16[8,4,16,256]{3,2,1,0:T(8,128)(2,1)S(1)}, bf16[64,128,128]{2,1,0:T(8,128)(2,1)S(1)}, bf16[64,128,384]{2,1,0:T(8,128)(2,1)S(1)}) custom-call(f32[64,256]{1,0:T(8,128)} %refs_0_.1, f32[12,64]{1,0:T(8,128)} %frames.1, s32[1,512]{1,0:T(1,128)} %bitcast.20, s32[1,512]{1,0:T(1,128)} %bitcast.21, s32[1,512]{1,0:T(1,128)} %bitcast.14, ...), custom_call_target="tpu_custom_call" | custom-call | tf_op jit(solution)/shard_map/pallas_call | solution.py:496
  30.1 0.0 copy-done
  30.1 0.0 copy-done.1
  30.1 0.0 copy-done.2
  30.1 0.0 copy-done.3
  30.1 0.0 copy-done.4
  30.1 0.0 copy-done.5
  30.1 0.0 copy-done.6
  30.1 0.0 copy-done.7
  30.1 0.0 copy-done.8
  30.1 0.0 copy-done.9
  30.2 0.0 copy-done.10
  30.2 0.0 copy-done.11
  30.2 0.0 copy-done.12
  30.2 14.3 %shard_map.311 = (f32[64,256]{1,0:T(8,128)}, f32[12,64]{1,0:T(8,128)}, bf16[64,128,128]{2,1,0:T(8,128)(2,1)}) custom-call(bf16[64,128,384]{2,1,0:T(8,128)(2,1)S(1)} %get-tuple-element.6.hidden_ref, bf16[64,128,128]{2,1,0:T(8,128)(2,1)S(1)} %get-tuple-element.7.pair_ref, bf16[512,256]{1,0:T(8,128)(2,1)S(1)} %bitcast.12, s32[1,512]{1,0:T(1,128)S(1)} %bitcast.15, ...), custom_call_target="tpu_custom_call" | custom-call | tf_op jit(solution)/shard_map/pallas_call | solution.py:721
Async XLA Ops:
  0.6 29.4 %copy-start = (bf16[2,256,768]{2,1,0:T(8,128)(2,1)S(1)}, bf16[2,256,768]{2,1,0:T(8,128)(2,1)}, u32[]{:S(2)}) copy-start(bf16[2,256,768]{2,1,0:T(8,128)(2,1)} %project.1) | copy-start | bytes 2359300
  0.6 29.4 %copy-start.1 = (bf16[256,768]{1,0:T(8,128)(2,1)S(1)}, bf16[256,768]{1,0:T(8,128)(2,1)}, u32[]{:S(2)}) copy-start(bf16[256,768]{1,0:T(8,128)(2,1)} %to_edge.1) | copy-start | bytes 1179652
  0.7 29.4 %copy-start.2 = (bf16[384,384]{1,0:T(8,128)(2,1)S(1)}, bf16[384,384]{1,0:T(8,128)(2,1)}, u32[]{:S(2)}) copy-start(bf16[384,384]{1,0:T(8,128)(2,1)} %second.1) | copy-start | bytes 884740
  0.7 29.4 %copy-start.3 = (bf16[2,256,256]{2,1,0:T(8,128)(2,1)S(1)}, bf16[2,256,256]{2,1,0:T(8,128)(2,1)}, u32[]{:S(2)}) copy-start(bf16[2,256,256]{2,1,0:T(8,128)(2,1)} %output.1) | copy-start | bytes 786436
  0.7 29.4 %copy-start.4 = (bf16[2,256,256]{2,1,0:T(8,128)(2,1)S(1)}, bf16[2,256,256]{2,1,0:T(8,128)(2,1)}, u32[]{:S(2)}) copy-start(bf16[2,256,256]{2,1,0:T(8,128)(2,1)} %expand.1) | copy-start | bytes 786436
  0.7 29.4 %copy-start.5 = (bf16[2,256,256]{2,1,0:T(8,128)(2,1)S(1)}, bf16[2,256,256]{2,1,0:T(8,128)(2,1)}, u32[]{:S(2)}) copy-start(bf16[2,256,256]{2,1,0:T(8,128)(2,1)} %shrink.1) | copy-start | bytes 786436
  0.7 29.4 %copy-start.6 = (bf16[384,128]{1,0:T(8,128)(2,1)S(1)}, bf16[384,128]{1,0:T(8,128)(2,1)}, u32[]{:S(2)}) copy-start(bf16[384,128]{1,0:T(8,128)(2,1)} %third.1) | copy-start | bytes 294916
  0.7 29.4 %copy-start.7 = (f32[12,64]{1,0:T(8,128)S(1)}, f32[12,64]{1,0:T(8,128)}, u32[]{:S(2)}) copy-start(f32[12,64]{1,0:T(8,128)} %frames.1) | copy-start | bytes 9220
  0.7 29.4 %copy-start.8 = (f32[256,6]{0,1:T(8,128)S(1)}, f32[256,6]{0,1:T(8,128)}, u32[]{:S(2)}) copy-start(f32[256,6]{0,1:T(8,128)} %param.53) | copy-start | bytes 18436
  0.7 29.4 %copy-start.9 = (s32[512]{0:T(512)S(1)}, s32[512]{0:T(512)}, u32[]{:S(2)}) copy-start(s32[512]{0:T(512)} %param.36) | copy-start | bytes 6148
  0.7 29.4 %copy-start.10 = (f32[2,2,256]{2,1,0:T(2,128)S(1)}, f32[2,2,256]{2,1,0:T(2,128)}, u32[]{:S(2)}) copy-start(f32[2,2,256]{2,1,0:T(2,128)} %scales.1) | copy-start | bytes 12292
  0.7 29.4 %copy-start.11 = (f32[2,384]{1,0:T(2,128)S(1)}, f32[2,384]{1,0:T(2,128)}, u32[]{:S(2)}) copy-start(f32[2,384]{1,0:T(2,128)} %biases.1) | copy-start | bytes 9220
  0.8 29.4 %copy-start.12 = (f32[128]{0:T(128)S(1)}, f32[128]{0:T(128)}, u32[]{:S(2)}) copy-start(f32[128]{0:T(128)} %param.59) | copy-start | bytes 1540

commit v4 on v3

--- a/solution.py
+++ b/solution.py
@@ -53,6 +53,8 @@
 def by_component(count):
     target = np.arange(3 * LANES)
     comp, rest = target // LANES, target % LANES
+    if LANES % (HEADS * count) == 0:
+        rest = rest % (HEADS * count)
     source = (rest // count * 3 + comp) * count + rest % count
     source = np.where(rest < HEADS * count, source, -1)
     return np.arange(HEADS * 3 * count)[:, None] == source[None, :]
@@ -74,6 +76,18 @@
         ],
         axis=1,
     )
+
+
+def fold(places):
+    first, second, third = (places[:, LANES * c : LANES * (c + 1)] for c in range(3))
+    low = iota((1, LANES), 1) < LANES // 2
+    return jnp.concatenate([jnp.where(low, first, second), jnp.where(low, third, 0.0)], axis=1)
+
+
+def head_of_fold(count):
+    lane = iota((HEADS, 2 * LANES), 1)
+    owner = lane % (LANES // 2) // count == iota((HEADS, 2 * LANES), 0)
+    return (owner & (lane < 3 * LANES // 2)).astype(jnp.float32)
 
 
 def head_of_lane(count):
@@ -203,10 +217,6 @@
 
     group = 8
     starts = list(range(0, rows, group))
-    early = starts[: len(starts) // 4]
-    late = starts[len(starts) // 4 :]
-    for start in early:
-        pair_rows(start, group)
 
     pl.semaphore_wait(barrier, len(along_pb) + len(along_ka))
     for slot in range(per):
@@ -240,7 +250,7 @@
             x_keys[slot] = x_send[...]
             f_keys[slot] = f_send[...]
 
-    for start in late:
+    for start in starts:
         pair_rows(start, group)
 
     own_columns = frame_columns(frames[...])
@@ -252,11 +262,11 @@
         load.wait()
     queries = dot(own, wq[...]).astype(jnp.bfloat16)
     spread = dot(perm_qk[...], point_query[...]).astype(jnp.bfloat16)
-    query_places = place(contract(own, spread, 1, 1), own_columns)
+    query_places = fold(place(contract(own, spread, 1, 1), own_columns))
     spread_key = dot(perm_qk[...], point_key[...]).astype(jnp.bfloat16)
     spread_value = dot(perm_v[...], point_value[...]).astype(jnp.bfloat16)
-    heads_qk = head_of_lane(QKP)
-    by_head = (query_places[:, None, :] * heads_qk[None]).reshape(rows * HEADS, 3 * LANES)
+    heads_qk = head_of_fold(QKP)
+    by_head = (query_places[:, None, :] * heads_qk[None]).reshape(rows * HEADS, 2 * LANES)
     query_square = jnp.sum(by_head * by_head, axis=-1, keepdims=True)
 
     for slot in range(per):
@@ -282,7 +292,7 @@
 
     key_rows = jnp.concatenate([x_keys[slot] for slot in range(per)], axis=0)
     key_columns = jnp.concatenate([frame_columns(f_keys[slot].astype(jnp.float32)) for slot in range(per)], axis=0)
-    key_places = place(contract(key_rows, spread_key, 1, 1), key_columns)
+    key_places = fold(place(contract(key_rows, spread_key, 1, 1), key_columns))
     cross = contract(by_head, key_places, 1, 1, precision=HIGHEST)
     key_square = contract(heads_qk, key_places * key_places, 1, 1, precision=HIGHEST)
     loads[16].wait()
@@ -339,7 +349,14 @@
     pair_out = jnp.stack([dot(rounded[i], pair_s[i]) for i in range(rows)], axis=0)
     value_places = place(contract(key_rows, spread_value, 1, 1), key_columns)
     heads_v = head_of_lane(VP)
-    points = dot(weights.reshape(rows * HEADS, keys), value_places, precision=HIGHEST)
+    value_high = value_places.astype(jnp.bfloat16)
+    value_low = (value_places - value_high.astype(jnp.float32)).astype(jnp.bfloat16)
+    weight_high = rounded.reshape(rows * HEADS, keys)
+    weight_low = (work_s[...] - weight_high.astype(jnp.float32)).astype(jnp.bfloat16)
+    points = dot(weight_high, value_high) + (
+        dot(weight_high, value_low) + dot(weight_low, value_high)
+    )
+    points = jnp.sum(points.reshape(rows, HEADS, 3 * LANES) * heads_v[None], axis=1)
 
     for copy in stats:
         copy.wait()
@@ -366,8 +383,7 @@
         features.append(work_s[pl.ds(head, rows, stride=HEADS), :])
     features = jnp.concatenate([piece.astype(jnp.bfloat16) for piece in features], axis=1)
     partial = dot(features, ow[: features.shape[1], :])
-    points = points.reshape(rows, HEADS, 3 * LANES) * (heads_v[None] * factor)
-    points = jnp.sum(points, axis=1)
+    points = points * contract(share, heads_v, 0, 0, precision=HIGHEST)[:rows]
     partial = jnp.concatenate([partial, points], axis=1)
     for a in range(n_ka):
         part_send[a] = partial[a * part : (a + 1) * part].astype(jnp.bfloat16)
@@ -421,22 +437,29 @@
     )
     mine[...] = layer_norm(states, scales[...]).astype(jnp.bfloat16)
     states_out[row, col] = mine[...]
+    def partner(distance):
+        other = row
+        for bit in (1 << k for k in range(n_pb.bit_length() - 1)):
+            if distance & bit:
+                other = other + bit * (1 - 2 * lax.rem(lax.div(row, bit), 2))
+        return other
+
     gathers = [
         pltpu.make_async_remote_copy(
             src_ref=mine,
             dst_ref=states_out.at[row, col],
-            send_sem=g_send_sem.at[d],
-            recv_sem=g_recv_sem.at[d],
-            device_id=peer,
+            send_sem=g_send_sem.at[distance - 1],
+            recv_sem=g_recv_sem.at[distance - 1],
+            device_id={"pb": partner(distance)},
             device_id_type=MESH,
         )
-        for d, peer in enumerate(along_pb)
+        for distance in range(1, n_pb)
     ]
-    for copy in gathers:
+    for copy in reversed(gathers):
         copy.start()
 
     def forward(distance):
-        source = lax.rem(row + n_pb - distance, n_pb)
+        source = partner(distance)
         copies = [
             pltpu.make_async_remote_copy(
                 src_ref=states_out.at[source, col] if distance else mine,
@@ -455,7 +478,7 @@
     spreads = forward(0)
     for start in starts[third:]:
         hidden_rows(start)
-    for distance in sorted(range(1, n_pb), key=lambda d: min(d, n_pb - d)):
+    for distance in range(1, n_pb):
         gathers[distance - 1].wait_recv()
         spreads += forward(distance)
     for copy in gathers:

time: 45 us -> 43.5 us (0.967)
  Pallas kernels: 43.6 us -> 42.1 us
    pallas_call x1, Pallas kernels: 29.3 us -> 27.8 us  [attend(): pl.pallas_call(functools.partial(attend_kernel, n_pb, n_ka), out_shape=(j...]
where the time goes in v4:
time: 43.5 us; the launch traced here: 43 us
  Pallas kernels  42.1 us (97%)
  between operations  0.85 us (2%)
    pallas_call x1, Pallas kernels, attend(): pl.pallas_call(functools.partial(attend_kernel, n_pb, n_ka), out_shape=(j...  27.8 us
    pallas_call x1, Pallas kernels, finish(): pl.pallas_call(functools.partial(finish_kernel, n_ka), grid=(rows // step...  14.3 us

profile of v4, /device:TPU:1, one launch (start us, length us, event | category | flops | bytes accessed | tf_op | source)
XLA Modules:
  0.0 43.0 jit_solution(1022010867423581104)
XLA Ops:
  0.6 0.0 copy-start
  0.6 0.0 copy-start.1
  0.7 0.0 copy-start.2
  0.7 0.0 copy-start.3
  0.7 0.0 copy-start.4
  0.7 0.0 copy-start.5
  0.7 0.0 copy-start.6
  0.7 0.0 copy-start.7
  0.7 0.0 copy-start.8
  0.7 0.0 copy-start.9
  0.7 0.0 copy-start.10
  0.7 0.0 copy-start.11
  0.8 0.0 copy-start.12
  0.8 27.8 %shard_map.310 = (bf16[8,4,16,256]{3,2,1,0:T(8,128)(2,1)S(1)}, bf16[64,128,128]{2,1,0:T(8,128)(2,1)S(1)}, bf16[64,128,384]{2,1,0:T(8,128)(2,1)S(1)}) custom-call(f32[64,256]{1,0:T(8,128)} %refs_0_.1, f32[12,64]{1,0:T(8,128)} %frames.1, s32[1,512]{1,0:T(1,128)} %bitcast.20, s32[1,512]{1,0:T(1,128)} %bitcast.21, s32[1,512]{1,0:T(1,128)} %bitcast.14, ...), custom_call_target="tpu_custom_call" | custom-call | tf_op jit(solution)/shard_map/pallas_call | solution.py:519
  28.6 0.0 copy-done
  28.6 0.0 copy-done.1
  28.6 0.0 copy-done.2
  28.6 0.0 copy-done.3
  28.6 0.0 copy-done.4
  28.6 0.0 copy-done.5
  28.6 0.0 copy-done.6
  28.6 0.0 copy-done.7
  28.7 0.0 copy-done.8
  28.7 0.0 copy-done.9
  28.7 0.0 copy-done.10
  28.7 0.0 copy-done.11
  28.7 0.0 copy-done.12
  28.7 14.3 %shard_map.311 = (f32[64,256]{1,0:T(8,128)}, f32[12,64]{1,0:T(8,128)}, bf16[64,128,128]{2,1,0:T(8,128)(2,1)}) custom-call(bf16[64,128,384]{2,1,0:T(8,128)(2,1)S(1)} %get-tuple-element.6.hidden_ref, bf16[64,128,128]{2,1,0:T(8,128)(2,1)S(1)} %get-tuple-element.7.pair_ref, bf16[512,256]{1,0:T(8,128)(2,1)S(1)} %bitcast.12, s32[1,512]{1,0:T(1,128)S(1)} %bitcast.15, ...), custom_call_target="tpu_custom_call" | custom-call | tf_op jit(solution)/shard_map/pallas_call | solution.py:744
Async XLA Ops:
  0.6 27.9 %copy-start = (bf16[2,256,768]{2,1,0:T(8,128)(2,1)S(1)}, bf16[2,256,768]{2,1,0:T(8,128)(2,1)}, u32[]{:S(2)}) copy-start(bf16[2,256,768]{2,1,0:T(8,128)(2,1)} %project.1) | copy-start | bytes 2359300
  0.6 27.9 %copy-start.1 = (bf16[256,768]{1,0:T(8,128)(2,1)S(1)}, bf16[256,768]{1,0:T(8,128)(2,1)}, u32[]{:S(2)}) copy-start(bf16[256,768]{1,0:T(8,128)(2,1)} %to_edge.1) | copy-start | bytes 1179652
  0.7 27.9 %copy-start.2 = (bf16[384,384]{1,0:T(8,128)(2,1)S(1)}, bf16[384,384]{1,0:T(8,128)(2,1)}, u32[]{:S(2)}) copy-start(bf16[384,384]{1,0:T(8,128)(2,1)} %second.1) | copy-start | bytes 884740
  0.7 27.9 %copy-start.3 = (bf16[2,256,256]{2,1,0:T(8,128)(2,1)S(1)}, bf16[2,256,256]{2,1,0:T(8,128)(2,1)}, u32[]{:S(2)}) copy-start(bf16[2,256,256]{2,1,0:T(8,128)(2,1)} %output.1) | copy-start | bytes 786436
  0.7 27.9 %copy-start.4 = (bf16[2,256,256]{2,1,0:T(8,128)(2,1)S(1)}, bf16[2,256,256]{2,1,0:T(8,128)(2,1)}, u32[]{:S(2)}) copy-start(bf16[2,256,256]{2,1,0:T(8,128)(2,1)} %expand.1) | copy-start | bytes 786436
  0.7 27.9 %copy-start.5 = (bf16[2,256,256]{2,1,0:T(8,128)(2,1)S(1)}, bf16[2,256,256]{2,1,0:T(8,128)(2,1)}, u32[]{:S(2)}) copy-start(bf16[2,256,256]{2,1,0:T(8,128)(2,1)} %shrink.1) | copy-start | bytes 786436
  0.7 27.9 %copy-start.6 = (bf16[384,128]{1,0:T(8,128)(2,1)S(1)}, bf16[384,128]{1,0:T(8,128)(2,1)}, u32[]{:S(2)}) copy-start(bf16[384,128]{1,0:T(8,128)(2,1)} %third.1) | copy-start | bytes 294916
  0.7 27.9 %copy-start.7 = (f32[12,64]{1,0:T(8,128)S(1)}, f32[12,64]{1,0:T(8,128)}, u32[]{:S(2)}) copy-start(f32[12,64]{1,0:T(8,128)} %frames.1) | copy-start | bytes 9220
  0.7 27.9 %copy-start.8 = (f32[256,6]{0,1:T(8,128)S(1)}, f32[256,6]{0,1:T(8,128)}, u32[]{:S(2)}) copy-start(f32[256,6]{0,1:T(8,128)} %param.53) | copy-start | bytes 18436
  0.7 27.9 %copy-start.9 = (s32[512]{0:T(512)S(1)}, s32[512]{0:T(512)}, u32[]{:S(2)}) copy-start(s32[512]{0:T(512)} %param.36) | copy-start | bytes 6148
  0.7 27.9 %copy-start.10 = (f32[2,2,256]{2,1,0:T(2,128)S(1)}, f32[2,2,256]{2,1,0:T(2,128)}, u32[]{:S(2)}) copy-start(f32[2,2,256]{2,1,0:T(2,128)} %scales.1) | copy-start | bytes 12292
  0.7 27.9 %copy-start.11 = (f32[2,384]{1,0:T(2,128)S(1)}, f32[2,384]{1,0:T(2,128)}, u32[]{:S(2)}) copy-start(f32[2,384]{1,0:T(2,128)} %biases.1) | copy-start | bytes 9220
  0.8 27.9 %copy-start.12 = (f32[128]{0:T(128)S(1)}, f32[128]{0:T(128)}, u32[]{:S(2)}) copy-start(f32[128]{0:T(128)} %param.59) | copy-start | bytes 1540
